TPU v7x, 32 devices: a whole 2x2x4 slice. The times are simulated.
32 devices in a mesh: gx: 8 (over y, x, core), gy: 4 (over z).
Axes of the slice: x: 2, y: 2, z: 4, core: 2. Of those that a mesh axis runs over, the one named last changes fastest.
Arguments:
- particle_count: int32 [8, 256, 1024], P(None, ('gx', 'gy')), may hold values from 0 to 12
- drag_coeff: float32 [8, 256, 1024], P(None, ('gx', 'gy')), may hold values from 0.05 to 2
- particle_velocity: float32 [3, 8, 256, 1024], P(None, None, ('gx', 'gy')), may hold values from -6 to 6
- fluid_velocity: float32 [3, 8, 256, 1024], P(None, None, 'gy', 'gx'), may hold values from -6 to 6
Outputs:
- pressure: float32 [8, 256, 1024], P(None, 'gy', 'gx')
- new_velocity: float32 [3, 8, 256, 1024], P(None, None, ('gx', 'gy'))
- pressure_gradient: float32 [3, 8, 256, 1024], P(None, None, ('gx', 'gy'))
All inputs are finite; a program needn't handle non-finite values.
Results may differ from a plain program's by a relative error of at most 0.00002.
Values sent between devices are 32-bit elements; how exact they have to be, the bound alone decides.
A program may use at most 64 MiB of HBM per device.

v0:
```python
import functools

import jax
import jax.numpy as jnp
from jax import lax
from jax.experimental import pallas as pl
from jax.experimental.pallas import tpu as pltpu
from jax.sharding import PartitionSpec as P

SWEEPS = 8
ROUNDS = (4, 4)

particle_volume = 0.05
time_step = 0.5
viscosity = 0.1


def kernel(
    K, G, R, NZ, NY, W,
    count_in, drag_in, pvel_in, fluid_in,
    press_out, vel_out, grad_out,
    fp, ub, cn, dr, pv, vo, total_w, wf, wr, wa, rh, pred, gr, fl, fr, t0, t1, pf, po,
    loc_sem, fh_send, fh_recv, s2_send, s2_recv,
    hal_send, hal_recv, pr_send, pr_recv, out_send, out_recv, *stages,
):
    H = max(ROUNDS)
    b = stages[0]
    C = G // K
    B = C * K
    x = lax.axis_index("gx")
    k = lax.axis_index("gy")
    place = x * K + k
    has_prev = place > 0
    has_next = place < G * K - 1
    prev_id = {"gx": jnp.where(k > 0, x, jnp.maximum(x - 1, 0)), "gy": lax.rem(k + K - 1, K)}
    next_id = {"gx": jnp.where(k < K - 1, x, jnp.minimum(x + 1, G - 1)), "gy": lax.rem(k + 1, K)}

    def remote(src, dst, ssem, rsem, to):
        return pltpu.make_async_remote_copy(
            src_ref=src, dst_ref=dst, send_sem=ssem, recv_sem=rsem, device_id=to, device_id_type=pl.DeviceIdType.MESH
        )

    rows = R * B

    local = [[] for _ in range(4)]
    for z in range(NZ):
        local[0].append(pltpu.make_async_copy(fluid_in.at[:, z], fp.at[:, 1:rows + 1, z], loc_sem.at[z]))
        local[1].append(pltpu.make_async_copy(count_in.at[z], cn.at[H:H + R, z], loc_sem.at[NZ + z]))
        local[2].append(pltpu.make_async_copy(drag_in.at[z], dr.at[:, z], loc_sem.at[2 * NZ + z]))
        local[3].append(pltpu.make_async_copy(pvel_in.at[:, z], pv.at[:, :, z], loc_sem.at[3 * NZ + z]))
    for copies in local:
        for copy in copies:
            copy.start()

    home = x // C
    barrier = pltpu.get_barrier_semaphore()

    def greet(to):
        pl.semaphore_signal(barrier, inc=1, device_id=to, device_id_type=pl.DeviceIdType.MESH)

    for d in range(1, K):
        greet({"gx": x, "gy": lax.rem(k + d, K)})
    @pl.when(has_prev)
    def _():
        greet(prev_id)

    @pl.when(has_next)
    def _():
        greet(next_id)

    for c in range(C):
        for j in range(K):
            @pl.when(jnp.logical_or(k * C + c != x, k != j))
            def _(c=c, j=j):
                greet({"gx": k * C + c, "gy": jnp.int32(j)})

    for t in range(G):
        @pl.when(jnp.logical_or(home != k, x != t))
        def _(t=t):
            greet({"gx": jnp.int32(t), "gy": home})

    one = jnp.int32(1)
    nothing = jnp.int32(0)
    heard = (
        K - 1 + G + C * K
        + jnp.where(has_prev, one, nothing)
        + jnp.where(has_next, one, nothing)
        - 2 * jnp.where(home == k, one, nothing)
    )

    @pl.when(k == 0)
    def _():
        fp[:, 0:1] = jnp.zeros((3, 1, NZ, W), jnp.float32)

    @pl.when(k == K - 1)
    def _():
        fp[:, rows + 1:rows + 2] = jnp.zeros((3, 1, NZ, W), jnp.float32)

    line = jnp.zeros((NZ, NY), jnp.float32)
    fl[0] = line
    fl[R + 1] = line
    edge = jnp.zeros((H, NZ, NY), jnp.float32)

    @pl.when(jnp.logical_not(has_prev))
    def _():
        fr[0] = line
        for buf in stages:
            buf[0:H] = edge

    @pl.when(jnp.logical_not(has_next))
    def _():
        fr[1] = line
        for buf in stages:
            buf[H + R:2 * H + R] = edge

    for copy in local[0]:
        copy.wait()
    pl.semaphore_wait(barrier, heard)

    up = {"gx": x, "gy": lax.rem(k + K - 1, K)}
    down = {"gx": x, "gy": lax.rem(k + 1, K)}
    to_up = remote(fp.at[:, 1:2], fp.at[:, rows + 1:rows + 2], fh_send.at[0], fh_recv.at[0], up)
    to_down = remote(fp.at[:, rows:rows + 1], fp.at[:, 0:1], fh_send.at[1], fh_recv.at[1], down)

    @pl.when(k > 0)
    def _():
        to_up.start()

    @pl.when(k < K - 1)
    def _():
        to_down.start()

    def part(at):
        return fp.at[:, pl.ds(at * R, R + 2)]

    def at_edge(c, j):
        low = (j == 0) if c == 0 else (j < 0)
        high = (j == K - 1) if c == C - 1 else (j < 0)
        return jnp.logical_or(low, high)

    columns = pl.ds(pl.multiple_of(x * W, W), W)

    sends = []
    for d in range(K):
        for c in range(C):
            j = lax.rem(k + d, K)
            target = k * C + c
            src = part(c * K + j)
            dst = ub.at[:, :, :, columns]
            far = remote(src, dst, s2_send.at[d * C + c], s2_recv.at[x], {"gx": target, "gy": j})
            near = pltpu.make_async_copy(src, dst, s2_recv.at[x])
            sends.append((c, j, far, near, jnp.logical_and(target == x, j == k)))

    def send_all(edges):
        for c, j, far, near, mine in sends:
            want = at_edge(c, j) if edges else jnp.logical_not(at_edge(c, j))

            @pl.when(jnp.logical_and(want, mine))
            def _(near=near):
                near.start()

            @pl.when(jnp.logical_and(want, jnp.logical_not(mine)))
            def _(far=far):
                far.start()

    send_all(False)

    @pl.when(k < K - 1)
    def _():
        to_up.wait_recv()

    @pl.when(k > 0)
    def _():
        to_down.wait_recv()

    send_all(True)

    halo_up = [remote(cn.at[H:2 * H], cn.at[H + R:2 * H + R], hal_send.at[0], hal_recv.at[0], prev_id)]
    halo_down = [remote(cn.at[R:R + H], cn.at[0:H], hal_send.at[1], hal_recv.at[1], next_id)]

    for copies in local[1:]:
        for copy in copies:
            copy.wait()

    @pl.when(has_prev)
    def _():
        for copy in halo_up:
            copy.start()

    @pl.when(has_next)
    def _():
        for copy in halo_down:
            copy.start()

    @pl.when(has_next)
    def _():
        for copy in halo_up:
            copy.wait_recv()

    @pl.when(has_prev)
    def _():
        for copy in halo_down:
            copy.wait_recv()

    lane = lax.broadcasted_iota(jnp.int32, (NZ, NY), 1)
    level = lax.broadcasted_iota(jnp.int32, (NZ, NY), 0)

    def above(v):
        return jnp.where(level < NZ - 1, pltpu.roll(v, NZ - 1, 0), 0.0)

    def below(v):
        return jnp.where(level > 0, pltpu.roll(v, 1, 0), 0.0)

    def right(v):
        return jnp.where(lane < NY - 1, pltpu.roll(v, NY - 1, 1), 0.0)

    def left(v):
        return jnp.where(lane > 0, pltpu.roll(v, 1, 1), 0.0)

    def plane_sum(v):
        return above(v) + below(v) + right(v) + left(v)

    def inside(i):
        at = place * R + i
        return jnp.logical_and(at >= 0, at < G * K * R)

    def voids_row(n, carry):
        v = 1.0 - cn[n].astype(jnp.float32) * particle_volume
        vo[n] = jnp.where(inside(n - H), v, 0.0)
        return carry

    lax.fori_loop(0, R + 2 * H, voids_row, 0)

    def weight_row(n, carry):
        v = vo[n]
        ws = 0.5 * (6.0 * v + vo[n - 1] + vo[n + 1] + plane_sum(v))
        total_w[n] = ws
        rh[n] = jnp.where(inside(n - H), 1.0 / ws, 0.0)
        wf[n] = 0.5 * (v + vo[n + 1])
        wr[n] = jnp.where(lane < NY - 1, 0.5 * (v + pltpu.roll(v, NY - 1, 1)), 0.0)
        wa[n] = jnp.where(level < NZ - 1, 0.5 * (v + pltpu.roll(v, NZ - 1, 0)), 0.0)
        return carry

    wf[0] = 0.5 * (vo[0] + vo[1])
    lax.fori_loop(1, R + 2 * H - 1, weight_row, 0)

    def weighted(n, p, pa, pb):
        r, a = wr[n], wa[n]
        across = r * pltpu.roll(p, NY - 1, 1) + pltpu.roll(r * p, 1, 1)
        upright = a * pltpu.roll(p, NZ - 1, 0) + pltpu.roll(a * p, 1, 0)
        return (wf[n - 1] * pa + wf[n] * pb) + (across + upright)

    for sender in range(G):
        spot = pl.ds(sender * W, W)
        here = {"gx": x, "gy": k}
        remote(part(0), ub.at[:, :, :, spot], s2_send.at[0], s2_recv.at[sender], here).wait_recv()

    def momentum_row(i, carry):
        v, ws = vo[H + i], total_w[H + i]
        drag = dr[i]
        below_line = 1.0 / (v + time_step * drag)
        for which in range(3):
            u = ub[which, i + 1]
            diffusion = weighted(H + i, u, ub[which, i], ub[which, i + 2]) - ws * u
            force = drag * pv[which, i]
            value = (v * u + (time_step * viscosity) * diffusion + time_step * force) * below_line
            pred[which, i] = value
            f = v * value
            if which == 0:
                fl[i + 1] = f
            elif which == 1:
                part_source = right(f) - left(f)
            else:
                b[H + i] = part_source + (above(f) - below(f))
        return carry

    lax.fori_loop(0, R, momentum_row, 0)

    def source_row(i, carry):
        b[H + i] = -(fl[i + 2] - fl[i] + b[H + i]) * rh[H + i]
        return carry

    lax.fori_loop(0, R, source_row, 0)

    def sweep(src, dst, reach):
        def row(n, carry):
            dst[n] = weighted(n, src[n], src[n - 1], src[n + 1]) * rh[n] + b[n]
            return carry

        lax.fori_loop(H - reach, H + R + reach, row, 0)

    def exchange(turn, depth):
        buf = stages[turn]
        upward = [
            remote(buf.at[H:H + depth], buf.at[H + R:H + R + depth], pr_send.at[2 * turn], pr_recv.at[2 * turn], prev_id)
        ]
        downward = [
            remote(
                buf.at[H + R - depth:H + R], buf.at[H - depth:H], pr_send.at[2 * turn + 1], pr_recv.at[2 * turn + 1], next_id
            )
        ]
        if turn == 0:
            upward.append(remote(fl.at[1], fr.at[1], hal_send.at[2], hal_recv.at[2], prev_id))
            downward.append(remote(fl.at[R], fr.at[0], hal_send.at[3], hal_recv.at[3], next_id))

        @pl.when(has_prev)
        def _():
            for copy in upward:
                copy.start()

        @pl.when(has_next)
        def _():
            for copy in downward:
                copy.start()

        @pl.when(has_prev)
        def _():
            for copy in upward:
                copy.wait_send()

        @pl.when(has_next)
        def _():
            for copy in downward:
                copy.wait_send()

        @pl.when(has_next)
        def _():
            for copy in upward:
                copy.wait_recv()

        @pl.when(has_prev)
        def _():
            for copy in downward:
                copy.wait_recv()

    done = 0
    for turn, depth in enumerate(ROUNDS):
        exchange(turn, depth)
        if turn == 0:
            b[H] = b[H] + fr[0] * rh[H]
            b[H + R - 1] = b[H + R - 1] - fr[1] * rh[H + R - 1]
            b[H - 1] = b[H - 1] - fl[1] * rh[H - 1]
            b[H + R] = b[H + R] + fl[R] * rh[H + R]
        src = stages[turn]
        for reach in range(depth - 1, -1, -1):
            done += 1
            if done == SWEEPS:
                break
            if done == SWEEPS - 1:
                dst = pf
            elif reach == 0:
                dst = stages[turn + 1]
            else:
                dst = t1 if src is t0 else t0
            sweep(src, dst, reach)
            src = dst

    block = lax.rem(x, C) * K + k
    spot_rows = pl.ds(block * R, R)
    outs = []
    for e in range(G):
        target = lax.rem(x + e, G)
        src = pf.at[H:H + R, :, pl.ds(pl.multiple_of(target * W, W), W)]
        dst = po.at[spot_rows]
        far = remote(src, dst, out_send.at[e], out_recv.at[block], {"gx": target, "gy": home})
        if e == 0:
            near = pltpu.make_async_copy(src, dst, out_recv.at[block])

            @pl.when(home != k)
            def _(far=far):
                far.start()

            @pl.when(home == k)
            def _(near=near):
                near.start()
        else:
            far.start()
        outs.append(far)

    def slope_row(i, carry):
        n = H + i
        p = pf[n]
        g0 = 0.5 * (pf[n + 1] - pf[n - 1])
        g1 = 0.5 * (right(p) - left(p))
        g2 = 0.5 * (above(p) - below(p))
        for which, g in enumerate((g0, g1, g2)):
            gr[which, i] = g
            pred[which, i] = pred[which, i] - time_step * g
        return carry

    lax.fori_loop(0, R, slope_row, 0)
    written = []
    for z in range(NZ):
        written.append(pltpu.make_async_copy(gr.at[:, :, z], grad_out.at[:, z], loc_sem.at[z]))
        written.append(pltpu.make_async_copy(pred.at[:, :, z], vel_out.at[:, z], loc_sem.at[NZ + z]))
    for copy in written:
        copy.start()

    @pl.when(k > 0)
    def _():
        to_up.wait_send()

    @pl.when(k < K - 1)
    def _():
        to_down.wait_send()

    for c, j, far, near, mine in sends:
        @pl.when(jnp.logical_not(mine))
        def _(far=far):
            far.wait_send()

    @pl.when(has_prev)
    def _():
        for copy in halo_up:
            copy.wait_send()

    @pl.when(has_next)
    def _():
        for copy in halo_down:
            copy.wait_send()

    for e, far in enumerate(outs):
        if e == 0:
            @pl.when(home != k)
            def _(far=far):
                far.wait_send()
        else:
            far.wait_send()

    for n in range(B):
        here = {"gx": x, "gy": k}
        remote(pf.at[H:H + R, :, 0:W], po.at[n * R:(n + 1) * R], out_send.at[0], out_recv.at[n], here).wait_recv()
    last = [pltpu.make_async_copy(po.at[:, z], press_out.at[z], loc_sem.at[2 * NZ + z]) for z in range(NZ)]
    for copy in last:
        copy.start()
    for copy in written + last:
        copy.wait()


def shards(K, G, particle_count, drag_coeff, particle_velocity, fluid_velocity):
    NZ, R, NY = particle_count.shape
    rows, W = fluid_velocity.shape[2:]
    C = G // K
    H = max(ROUNDS)
    f32 = jnp.float32

    dma = pltpu.SemaphoreType.DMA
    pad = (R + 2 * H, NZ, NY)
    scratch = [
        pltpu.VMEM((3, rows + 2, NZ, W), f32),
        pltpu.VMEM((3, R + 2, NZ, NY), f32),
        pltpu.VMEM(pad, jnp.int32),
        pltpu.VMEM((R, NZ, NY), f32),
        pltpu.VMEM((3, R, NZ, NY), f32),
        *[pltpu.VMEM(pad, f32) for _ in range(6)],
        pltpu.VMEM((3, R, NZ, NY), f32),
        pltpu.VMEM((3, R, NZ, NY), f32),
        pltpu.VMEM((R + 2, NZ, NY), f32),
        pltpu.VMEM((2, NZ, NY), f32),
        pltpu.VMEM(pad, f32),
        pltpu.VMEM(pad, f32),
        pltpu.VMEM(pad, f32),
        pltpu.VMEM((rows, NZ, W), f32),
        dma((4 * NZ,)), dma((2,)), dma((2,)),
        dma((K * C,)), dma((G,)),
        dma((4,)), dma((4,)), dma((2 * len(ROUNDS),)), dma((2 * len(ROUNDS),)), dma((G,)), dma((C * K,)),
        *[pltpu.VMEM(pad, f32) for _ in ROUNDS],
    ]
    anywhere = pl.BlockSpec(memory_space=pl.ANY)
    return pl.pallas_call(
        functools.partial(kernel, K, G, R, NZ, NY, W),
        out_shape=(
            jax.ShapeDtypeStruct((NZ, rows, W), f32),
            jax.ShapeDtypeStruct((3, NZ, R, NY), f32),
            jax.ShapeDtypeStruct((3, NZ, R, NY), f32),
        ),
        in_specs=[anywhere] * 4,
        out_specs=(anywhere, anywhere, anywhere),
        scratch_shapes=scratch,
        compiler_params=pltpu.CompilerParams(collective_id=0, has_side_effects=True, vmem_limit_bytes=67043328),
    )(particle_count, drag_coeff, particle_velocity, fluid_velocity)


def solution(mesh):
    placed = (
        P(None, ("gx", "gy"), None),
        P(None, ("gx", "gy"), None),
        P(None, None, ("gx", "gy"), None),
        P(None, None, "gy", "gx"),
    )
    return jax.shard_map(
        functools.partial(shards, mesh.shape["gy"], mesh.shape["gx"]),
        mesh=mesh,
        in_specs=placed,
        out_specs=(
            P(None, "gy", "gx"),
            P(None, None, ("gx", "gy"), None),
            P(None, None, ("gx", "gy"), None),
        ),
        check_vma=False,
    )
```

profile of v0, /device:TPU:0, one launch (start us, length us, event | category | flops | bytes accessed | tf_op | source)
XLA Modules:
  0.0 82.8 jit_solution(12172470120604523470)
XLA Ops:
  0.6 77.4 %shard_map.67 = (f32[8,64,128]{2,1,0:T(8,128)}, f32[3,8,8,1024]{3,2,1,0:T(8,128)}, f32[3,8,8,1024]{3,2,1,0:T(8,128)}) custom-call(s32[8,8,1024]{2,1,0:T(8,128)} %count_in.1, f32[8,8,1024]{2,1,0:T(8,128)} %drag_in.1, f32[3,8,8,1024]{3,2,1,0:T(8,128)} %pvel_in.1, f32[3,8,64,128]{3,2,1,0:T(8,128)} %fluid_in.1), custom_call_target="tpu_custom_call" | custom-call | tf_op jit(solution)/shard_map/pallas_call | solution.py:470
  78.1 1.7 %copy.10 = f32[8,64,128]{2,1,0:T(8,128)} copy(f32[8,64,128]{2,1,0:T(8,128)} %get-tuple-element.6) | data formatting | bytes 524288
  79.8 0.0 copy-start
  79.8 2.2 %copy.11 = f32[3,8,8,1024]{3,2,1,0:T(8,128)} copy(f32[3,8,8,1024]{3,2,1,0:T(8,128)} %get-tuple-element.7) | data formatting | bytes 1572864
  81.9 0.0 copy-done
  81.9 0.9 %copy.12 = f32[3,8,8,1024]{3,2,1,0:T(8,128)} copy(f32[3,8,8,1024]{3,2,1,0:T(8,128)S(1)} %copy-done) | data formatting | bytes 1572864
Async XLA Ops:
  79.8 2.2 %copy-start = (f32[3,8,8,1024]{3,2,1,0:T(8,128)S(1)}, f32[3,8,8,1024]{3,2,1,0:T(8,128)}, u32[]{:S(2)}) copy-start(f32[3,8,8,1024]{3,2,1,0:T(8,128)} %get-tuple-element.8) | copy-start | bytes 2359300
where the time goes:
time: 83 us; the launch traced here: 82.8 us
  Pallas kernels  77.4 us (93%)
  local copies, waits for them, and re-layouts  4.72 us (6%)
    pallas_call x1, Pallas kernels, shards(): pl.pallas_call(functools.partial(kernel, K, G, R, NZ, NY, W), out_shape=(...  77.4 us
    unnamed x5, local copies, waits for them, and re-layouts  4.72 us

commit v1 on v0

--- a/solution.py
+++ b/solution.py
@@ -19,9 +19,9 @@
     K, G, R, NZ, NY, W,
     count_in, drag_in, pvel_in, fluid_in,
     press_out, vel_out, grad_out,
-    fp, ub, cn, dr, pv, vo, total_w, wf, wr, wa, rh, pred, gr, fl, fr, t0, t1, pf, po,
+    fp, ub, cn, dr, pv, vo, total_w, wf, wr, wa, rh, pred, gr, fl, fr, t0, t1, pf, rl, po,
     loc_sem, fh_send, fh_recv, s2_send, s2_recv,
-    hal_send, hal_recv, pr_send, pr_recv, out_send, out_recv, *stages,
+    hal_send, hal_recv, pr_send, pr_recv, out_send, out_recv, up_send, up_recv, *stages,
 ):
     H = max(ROUNDS)
     b = stages[0]
@@ -79,10 +79,13 @@
         def _(t=t):
             greet({"gx": jnp.int32(t), "gy": home})
 
+    for d in range(1, G):
+        greet({"gx": lax.rem(x + d, G), "gy": k})
+
     one = jnp.int32(1)
     nothing = jnp.int32(0)
     heard = (
-        K - 1 + G + C * K
+        K - 1 + G - 1 + G + C * K
         + jnp.where(has_prev, one, nothing)
         + jnp.where(has_next, one, nothing)
         - 2 * jnp.where(home == k, one, nothing)
@@ -355,27 +358,15 @@
             sweep(src, dst, reach)
             src = dst
 
-    block = lax.rem(x, C) * K + k
-    spot_rows = pl.ds(block * R, R)
     outs = []
-    for e in range(G):
+    for e in range(1, G):
         target = lax.rem(x + e, G)
         src = pf.at[H:H + R, :, pl.ds(pl.multiple_of(target * W, W), W)]
-        dst = po.at[spot_rows]
-        far = remote(src, dst, out_send.at[e], out_recv.at[block], {"gx": target, "gy": home})
-        if e == 0:
-            near = pltpu.make_async_copy(src, dst, out_recv.at[block])
-
-            @pl.when(home != k)
-            def _(far=far):
-                far.start()
-
-            @pl.when(home == k)
-            def _(near=near):
-                near.start()
-        else:
-            far.start()
-        outs.append(far)
+        outs.append(remote(src, rl.at[x], out_send.at[e], out_recv.at[x], {"gx": target, "gy": k}))
+    kept = pltpu.make_async_copy(pf.at[H:H + R, :, columns], rl.at[x], out_recv.at[x])
+    kept.start()
+    for copy in outs:
+        copy.start()
 
     def slope_row(i, carry):
         n = H + i
@@ -419,18 +410,38 @@
         for copy in halo_down:
             copy.wait_send()
 
-    for e, far in enumerate(outs):
-        if e == 0:
-            @pl.when(home != k)
-            def _(far=far):
-                far.wait_send()
-        else:
+    here = {"gx": x, "gy": k}
+    rises = []
+    for d in range(K):
+        to = lax.rem(home + d, K)
+        for c in range(C):
+            slot = to * C + c
+            remote(pf.at[H:H + R, :, 0:W], rl.at[slot], out_send.at[0], out_recv.at[slot], here).wait_recv()
+        src = rl.at[pl.ds(to * C, C)]
+        far = remote(src, po.at[:, k], up_send.at[d], up_recv.at[k], {"gx": x, "gy": to})
+        near = pltpu.make_async_copy(src, po.at[:, k], up_recv.at[k])
+
+        @pl.when(to != k)
+        def _(far=far):
+            far.start()
+
+        @pl.when(to == k)
+        def _(near=near):
+            near.start()
+
+        rises.append((to, far))
+
+    for copy in outs:
+        copy.wait_send()
+
+    for to, far in rises:
+        @pl.when(to != k)
+        def _(far=far):
             far.wait_send()
 
-    for n in range(B):
-        here = {"gx": x, "gy": k}
-        remote(pf.at[H:H + R, :, 0:W], po.at[n * R:(n + 1) * R], out_send.at[0], out_recv.at[n], here).wait_recv()
-    last = [pltpu.make_async_copy(po.at[:, z], press_out.at[z], loc_sem.at[2 * NZ + z]) for z in range(NZ)]
+    for j in range(K):
+        remote(rl.at[0:C], po.at[:, j], up_send.at[0], up_recv.at[j], here).wait_recv()
+    last = [pltpu.make_async_copy(po.at[:, :, :, z], press_out.at[z], loc_sem.at[2 * NZ + z]) for z in range(NZ)]
     for copy in last:
         copy.start()
     for copy in written + last:
@@ -460,17 +471,18 @@
         pltpu.VMEM(pad, f32),
         pltpu.VMEM(pad, f32),
         pltpu.VMEM(pad, f32),
-        pltpu.VMEM((rows, NZ, W), f32),
+        pltpu.VMEM((G, R, NZ, W), f32),
+        pltpu.VMEM((C, K, R, NZ, W), f32),
         dma((4 * NZ,)), dma((2,)), dma((2,)),
         dma((K * C,)), dma((G,)),
-        dma((4,)), dma((4,)), dma((2 * len(ROUNDS),)), dma((2 * len(ROUNDS),)), dma((G,)), dma((C * K,)),
+        dma((4,)), dma((4,)), dma((2 * len(ROUNDS),)), dma((2 * len(ROUNDS),)), dma((G,)), dma((G,)), dma((K,)), dma((K,)),
         *[pltpu.VMEM(pad, f32) for _ in ROUNDS],
     ]
     anywhere = pl.BlockSpec(memory_space=pl.ANY)
-    return pl.pallas_call(
+    pressure, velocity, slopes = pl.pallas_call(
         functools.partial(kernel, K, G, R, NZ, NY, W),
         out_shape=(
-            jax.ShapeDtypeStruct((NZ, rows, W), f32),
+            jax.ShapeDtypeStruct((NZ, C, K, R, W), f32),
             jax.ShapeDtypeStruct((3, NZ, R, NY), f32),
             jax.ShapeDtypeStruct((3, NZ, R, NY), f32),
         ),
@@ -479,6 +491,7 @@
         scratch_shapes=scratch,
         compiler_params=pltpu.CompilerParams(collective_id=0, has_side_effects=True, vmem_limit_bytes=67043328),
     )(particle_count, drag_coeff, particle_velocity, fluid_velocity)
+    return pressure.reshape(NZ, rows, W), velocity, slopes
 
 
 def solution(mesh):

time: 83 us -> 80.3 us (0.967)
  the two profiles are of different devices: /device:TPU:0 before, /device:TPU:13 now
where the time goes in v1:
time: 80.3 us; the launch traced here: 80.1 us
  Pallas kernels  74.7 us (93%)
  local copies, waits for them, and re-layouts  4.72 us (6%)
    pallas_call x1, Pallas kernels, shards(): pl.pallas_call(functools.partial(kernel, K, G, R, NZ, NY, W), out_shape=(...  74.7 us
    unnamed x5, local copies, waits for them, and re-layouts  4.72 us

profile of v1, /device:TPU:13, one launch (start us, length us, event | category | flops | bytes accessed | tf_op | source)
XLA Modules:
  0.0 80.1 jit_solution(9137357612883871544)
XLA Ops:
  0.6 74.7 %shard_map.67 = (f32[8,2,4,8,128]{4,3,2,1,0:T(8,128)}, f32[3,8,8,1024]{3,2,1,0:T(8,128)}, f32[3,8,8,1024]{3,2,1,0:T(8,128)}) custom-call(s32[8,8,1024]{2,1,0:T(8,128)} %count_in.1, f32[8,8,1024]{2,1,0:T(8,128)} %drag_in.1, f32[3,8,8,1024]{3,2,1,0:T(8,128)} %pvel_in.1, f32[3,8,64,128]{3,2,1,0:T(8,128)} %fluid_in.1), custom_call_target="tpu_custom_call" | custom-call | tf_op jit(solution)/shard_map/pallas_call | solution.py:482
  75.4 1.7 %copy.10 = f32[8,64,128]{2,1,0:T(8,128)} copy(f32[8,64,128]{2,1,0:T(8,128)} %bitcast.1) | data formatting | bytes 524288
  77.0 0.0 copy-start
  77.0 2.2 %copy.11 = f32[3,8,8,1024]{3,2,1,0:T(8,128)} copy(f32[3,8,8,1024]{3,2,1,0:T(8,128)} %get-tuple-element.13) | data formatting | bytes 1572864
  79.2 0.0 copy-done
  79.2 0.9 %copy.12 = f32[3,8,8,1024]{3,2,1,0:T(8,128)} copy(f32[3,8,8,1024]{3,2,1,0:T(8,128)S(1)} %copy-done) | data formatting | bytes 1572864
Async XLA Ops:
  77.0 2.2 %copy-start = (f32[3,8,8,1024]{3,2,1,0:T(8,128)S(1)}, f32[3,8,8,1024]{3,2,1,0:T(8,128)}, u32[]{:S(2)}) copy-start(f32[3,8,8,1024]{3,2,1,0:T(8,128)} %get-tuple-element.14) | copy-start | bytes 2359300

commit v2 on v1

--- a/solution.py
+++ b/solution.py
@@ -19,12 +19,13 @@
     K, G, R, NZ, NY, W,
     count_in, drag_in, pvel_in, fluid_in,
     press_out, vel_out, grad_out,
-    fp, ub, cn, dr, pv, vo, total_w, wf, wr, wa, rh, pred, gr, fl, fr, t0, t1, pf, rl, po,
+    fp, ub, cn, dr, pv, vo, total_w, wf, wr, wa, rh, pred, gr, fl, fr, eb, lv, rl, po,
     loc_sem, fh_send, fh_recv, s2_send, s2_recv,
-    hal_send, hal_recv, pr_send, pr_recv, out_send, out_recv, up_send, up_recv, *stages,
+    hal_send, hal_recv, b_send, b_recv, p_send, p_recv, out_send, out_recv, up_send, up_recv,
 ):
     H = max(ROUNDS)
-    b = stages[0]
+    first, last_level = ROUNDS[0], SWEEPS - 1
+    b, pf = lv.at[0], lv.at[last_level]
     C = G // K
     B = C * K
     x = lax.axis_index("gx")
@@ -107,14 +108,14 @@
     @pl.when(jnp.logical_not(has_prev))
     def _():
         fr[0] = line
-        for buf in stages:
-            buf[0:H] = edge
+        lv[0, 0:H] = edge
+        lv[first, 0:H] = edge
 
     @pl.when(jnp.logical_not(has_next))
     def _():
         fr[1] = line
-        for buf in stages:
-            buf[H + R:2 * H + R] = edge
+        lv[0, H + R:2 * H + R] = edge
+        lv[first, H + R:2 * H + R] = edge
 
     for copy in local[0]:
         copy.wait()
@@ -258,105 +259,155 @@
         here = {"gx": x, "gy": k}
         remote(part(0), ub.at[:, :, :, spot], s2_send.at[0], s2_recv.at[sender], here).wait_recv()
 
-    def momentum_row(i, carry):
-        v, ws = vo[H + i], total_w[H + i]
-        drag = dr[i]
-        below_line = 1.0 / (v + time_step * drag)
+    def pass_on(src_up, dst_up, src_down, dst_down, ssem, rsem, at):
+        return (
+            remote(src_up, dst_up, ssem.at[0, at], rsem.at[0, at], prev_id),
+            remote(src_down, dst_down, ssem.at[1, at], rsem.at[1, at], next_id),
+        )
+
+    def flux_rows():
+        return pass_on(fl.at[1], fr.at[1], fl.at[R], fr.at[0], b_send, b_recv, 0)
+
+    def level_rows(buf, s, ssem, rsem, at):
+        return pass_on(buf.at[H + s], buf.at[H + R + s], buf.at[H + R - 1 - s], buf.at[H - 1 - s], ssem, rsem, at)
+
+    def base_rows(s):
+        return level_rows(b, s, b_send, b_recv, s + 1)
+
+    def edge_rows():
+        return pass_on(eb.at[0], b.at[H + R], eb.at[1], b.at[H - 1], b_send, b_recv, 1)
+
+    def mid_rows(s):
+        return level_rows(lv.at[first], s, p_send, p_recv, s)
+
+    def launch(copies):
+        @pl.when(has_prev)
+        def _():
+            copies[0].start()
+
+        @pl.when(has_next)
+        def _():
+            copies[1].start()
+
+    def arrived(copies):
+        @pl.when(has_next)
+        def _():
+            copies[0].wait_recv()
+
+        @pl.when(has_prev)
+        def _():
+            copies[1].wait_recv()
+
+    def sent(copies):
+        @pl.when(has_prev)
+        def _():
+            copies[0].wait_send()
+
+        @pl.when(has_next)
+        def _():
+            copies[1].wait_send()
+
+    def momentum(i, which):
+        v, ws, drag, u = vo[H + i], total_w[H + i], dr[i], ub[which, i + 1]
+        diffusion = weighted(H + i, u, ub[which, i], ub[which, i + 2]) - ws * u
+        force = drag * pv[which, i]
+        return (v * u + (time_step * viscosity) * diffusion + time_step * force) / (v + time_step * drag)
+
+    def finish(i):
+        b[H + i] = -(fl[i + 2] - fl[i] + b[H + i]) * rh[H + i]
+
+    def momentum_step(s, carry):
+        pair = (s, R - 1 - s)
         for which in range(3):
-            u = ub[which, i + 1]
-            diffusion = weighted(H + i, u, ub[which, i], ub[which, i + 2]) - ws * u
-            force = drag * pv[which, i]
-            value = (v * u + (time_step * viscosity) * diffusion + time_step * force) * below_line
-            pred[which, i] = value
-            f = v * value
+            values = [momentum(i, which) for i in pair]
+            for i, value in zip(pair, values):
+                pred[which, i] = value
+            flux = [vo[H + i] * value for i, value in zip(pair, values)]
             if which == 0:
-                fl[i + 1] = f
+                for i, f in zip(pair, flux):
+                    fl[i + 1] = f
+
+                @pl.when(s == 0)
+                def _():
+                    launch(flux_rows())
+
             elif which == 1:
-                part_source = right(f) - left(f)
+                part_source = [right(f) - left(f) for f in flux]
             else:
-                b[H + i] = part_source + (above(f) - below(f))
+                for i, f, part in zip(pair, flux, part_source):
+                    b[H + i] = part + (above(f) - below(f))
+
+        @pl.when(s > 0)
+        def _():
+            finish(s - 1)
+            finish(R - s)
+
+            @pl.when(s == 1)
+            def _():
+                eb[0] = b[H]
+                eb[1] = b[H + R - 1]
+                launch(edge_rows())
+
+            @pl.when(jnp.logical_and(s > 1, s <= H))
+            def _():
+                launch(base_rows(s - 1))
+
         return carry
 
-    lax.fori_loop(0, R, momentum_row, 0)
-
-    def source_row(i, carry):
-        b[H + i] = -(fl[i + 2] - fl[i] + b[H + i]) * rh[H + i]
-        return carry
-
-    lax.fori_loop(0, R, source_row, 0)
-
-    def sweep(src, dst, reach):
-        def row(n, carry):
-            dst[n] = weighted(n, src[n], src[n - 1], src[n + 1]) * rh[n] + b[n]
+    half = R // 2
+    lax.fori_loop(0, half, momentum_step, 0)
+    finish(half - 1)
+    finish(R - half)
+    if half <= H:
+        launch(base_rows(half - 1))
+
+    def sweep_pair(l, lo):
+        hi = 2 * H + R - 1 - lo
+        values = [
+            weighted(n, lv[l - 1, n], lv[l - 1, n - 1], lv[l - 1, n + 1]) * rh[n] + b[n] for n in (lo, hi)
+        ]
+        lv[l, lo] = values[0]
+        lv[l, hi] = values[1]
+
+    def diagonal(j, start, stop):
+        def level(l, carry):
+            sweep_pair(l, l + (H - j))
             return carry
 
-        lax.fori_loop(H - reach, H + R + reach, row, 0)
-
-    def exchange(turn, depth):
-        buf = stages[turn]
-        upward = [
-            remote(buf.at[H:H + depth], buf.at[H + R:H + R + depth], pr_send.at[2 * turn], pr_recv.at[2 * turn], prev_id)
-        ]
-        downward = [
-            remote(
-                buf.at[H + R - depth:H + R], buf.at[H - depth:H], pr_send.at[2 * turn + 1], pr_recv.at[2 * turn + 1], next_id
-            )
-        ]
-        if turn == 0:
-            upward.append(remote(fl.at[1], fr.at[1], hal_send.at[2], hal_recv.at[2], prev_id))
-            downward.append(remote(fl.at[R], fr.at[0], hal_send.at[3], hal_recv.at[3], next_id))
-
-        @pl.when(has_prev)
-        def _():
-            for copy in upward:
-                copy.start()
-
-        @pl.when(has_next)
-        def _():
-            for copy in downward:
-                copy.start()
-
-        @pl.when(has_prev)
-        def _():
-            for copy in upward:
-                copy.wait_send()
-
-        @pl.when(has_next)
-        def _():
-            for copy in downward:
-                copy.wait_send()
-
-        @pl.when(has_next)
-        def _():
-            for copy in upward:
-                copy.wait_recv()
-
-        @pl.when(has_prev)
-        def _():
-            for copy in downward:
-                copy.wait_recv()
-
-    done = 0
-    for turn, depth in enumerate(ROUNDS):
-        exchange(turn, depth)
-        if turn == 0:
+        lax.fori_loop(start, stop, level, 0)
+
+    def rows_of(l, start, stop):
+        def row(lo, carry):
+            sweep_pair(l, lo)
+            return carry
+
+        lax.fori_loop(H + start, H + stop, row, 0)
+
+    for j in range(2 - half, H + 1):
+        if j == 0:
+            arrived(flux_rows())
             b[H] = b[H] + fr[0] * rh[H]
             b[H + R - 1] = b[H + R - 1] - fr[1] * rh[H + R - 1]
-            b[H - 1] = b[H - 1] - fl[1] * rh[H - 1]
-            b[H + R] = b[H + R] + fl[R] * rh[H + R]
-        src = stages[turn]
-        for reach in range(depth - 1, -1, -1):
-            done += 1
-            if done == SWEEPS:
-                break
-            if done == SWEEPS - 1:
-                dst = pf
-            elif reach == 0:
-                dst = stages[turn + 1]
-            else:
-                dst = t1 if src is t0 else t0
-            sweep(src, dst, reach)
-            src = dst
+        elif j > 0:
+            arrived(base_rows(j - 1))
+            if j == 1:
+                b[H - 1] = b[H - 1] - fl[1] * rh[H - 1]
+                b[H + R] = b[H + R] + fl[R] * rh[H + R]
+        stop = min(last_level, j + half - 1) + 1
+        diagonal(j, 1, min(stop, first + 1))
+        if j > 0:
+            launch(mid_rows(first - j))
+        if stop > first + 1:
+            diagonal(j, first + 1, stop)
+
+    depth = last_level - first
+    for s in range(first - 1, 0, -1):
+        arrived(mid_rows(s))
+    rows_of(first + 1, -depth, 1 - depth)
+    arrived(mid_rows(0))
+    for l in range(first + 1, last_level + 1):
+        low = l - last_level - 1 + (1 if l in (first + 1, last_level) else 0)
+        rows_of(l, low, l - H)
 
     outs = []
     for e in range(1, G):
@@ -367,6 +418,8 @@
     kept.start()
     for copy in outs:
         copy.start()
+
+    rows_of(last_level, -1, 0)
 
     def slope_row(i, carry):
         n = H + i
@@ -431,6 +484,9 @@
 
         rises.append((to, far))
 
+    for copies in [flux_rows(), edge_rows()] + [base_rows(i) for i in range(1, H)] + [mid_rows(i) for i in range(first)]:
+        sent(copies)
+
     for copy in outs:
         copy.wait_send()
 
@@ -445,6 +501,15 @@
     for copy in last:
         copy.start()
     for copy in written + last:
+        copy.wait()
+
+
+def settle(*refs):
+    n = len(refs) // 2
+    copies = [pltpu.make_async_copy(refs[i], refs[n + i], refs[-1].at[i]) for i in range(n)]
+    for copy in copies:
+        copy.start()
+    for copy in copies:
         copy.wait()
 
 
@@ -468,15 +533,13 @@
         pltpu.VMEM((3, R, NZ, NY), f32),
         pltpu.VMEM((R + 2, NZ, NY), f32),
         pltpu.VMEM((2, NZ, NY), f32),
-        pltpu.VMEM(pad, f32),
-        pltpu.VMEM(pad, f32),
-        pltpu.VMEM(pad, f32),
+        pltpu.VMEM((2, NZ, NY), f32),
+        pltpu.VMEM((SWEEPS,) + pad, f32),
         pltpu.VMEM((G, R, NZ, W), f32),
         pltpu.VMEM((C, K, R, NZ, W), f32),
         dma((4 * NZ,)), dma((2,)), dma((2,)),
         dma((K * C,)), dma((G,)),
-        dma((4,)), dma((4,)), dma((2 * len(ROUNDS),)), dma((2 * len(ROUNDS),)), dma((G,)), dma((G,)), dma((K,)), dma((K,)),
-        *[pltpu.VMEM(pad, f32) for _ in ROUNDS],
+        dma((2,)), dma((2,)), dma((2, H + 1)), dma((2, H + 1)), dma((2, H)), dma((2, H)), dma((G,)), dma((G,)), dma((K,)), dma((K,)),
     ]
     anywhere = pl.BlockSpec(memory_space=pl.ANY)
     pressure, velocity, slopes = pl.pallas_call(
@@ -491,7 +554,14 @@
         scratch_shapes=scratch,
         compiler_params=pltpu.CompilerParams(collective_id=0, has_side_effects=True, vmem_limit_bytes=67043328),
     )(particle_count, drag_coeff, particle_velocity, fluid_velocity)
-    return pressure.reshape(NZ, rows, W), velocity, slopes
+    found = (pressure.reshape(NZ, rows, W), velocity, slopes)
+    return pl.pallas_call(
+        settle,
+        out_shape=[jax.ShapeDtypeStruct(v.shape, f32) for v in found],
+        in_specs=[pl.BlockSpec(memory_space=pltpu.VMEM)] * 3,
+        out_specs=[anywhere] * 3,
+        scratch_shapes=[dma((3,))],
+    )(*found)
 
 
 def solution(mesh):

time: 80.3 us -> 70.4 us (0.88)
  the two profiles are of different devices: /device:TPU:13 before, /device:TPU:0 now
where the time goes in v2:
time: 70.4 us; the launch traced here: 69.2 us
  Pallas kernels  68.6 us (97%)
    pallas_call x1, Pallas kernels, shards(): pl.pallas_call(functools.partial(kernel, K, G, R, NZ, NY, W), out_shape=(...  65.9 us
    pallas_call x1, Pallas kernels, shards(): pl.pallas_call(settle, out_shape=[jax.ShapeDtypeStruct(v.shape, f32) for...  2.7 us

profile of v2, /device:TPU:0, one launch (start us, length us, event | category | flops | bytes accessed | tf_op | source)
XLA Modules:
  0.0 69.2 jit_solution(15648274010158624204)
XLA Ops:
  0.6 65.9 %shard_map.67 = (f32[8,2,4,8,128]{4,3,2,1,0:T(8,128)}, f32[3,8,8,1024]{3,2,1,0:T(8,128)}, f32[3,8,8,1024]{3,2,1,0:T(8,128)}) custom-call(s32[8,8,1024]{2,1,0:T(8,128)} %count_in.1, f32[8,8,1024]{2,1,0:T(8,128)} %drag_in.1, f32[3,8,8,1024]{3,2,1,0:T(8,128)} %pvel_in.1, f32[3,8,64,128]{3,2,1,0:T(8,128)} %fluid_in.1), custom_call_target="tpu_custom_call" | custom-call | tf_op jit(solution)/shard_map/pallas_call | solution.py:545
  66.5 2.7 %shard_map.68 = (f32[8,64,128]{2,1,0:T(8,128)}, f32[3,8,8,1024]{3,2,1,0:T(8,128)}, f32[3,8,8,1024]{3,2,1,0:T(8,128)}) custom-call(f32[8,64,128]{2,1,0:T(8,128)} %bitcast.1, f32[3,8,8,1024]{3,2,1,0:T(8,128)} %get-tuple-element.7.refs_1_, f32[3,8,8,1024]{3,2,1,0:T(8,128)} %get-tuple-element.8.refs_2_), custom_call_target="tpu_custom_call" | custom-call | tf_op jit(solution)/shard_map/pallas_call | solution.py:558

commit v3 on v2

--- a/solution.py
+++ b/solution.py
@@ -20,7 +20,7 @@
     count_in, drag_in, pvel_in, fluid_in,
     press_out, vel_out, grad_out,
     fp, ub, cn, dr, pv, vo, total_w, wf, wr, wa, rh, pred, gr, fl, fr, eb, lv, rl, po,
-    loc_sem, fh_send, fh_recv, s2_send, s2_recv,
+    loc_sem, row_send, row_recv, s2_send, s2_recv,
     hal_send, hal_recv, b_send, b_recv, p_send, p_recv, out_send, out_recv, up_send, up_recv,
 ):
     H = max(ROUNDS)
@@ -45,62 +45,35 @@
 
     local = [[] for _ in range(4)]
     for z in range(NZ):
-        local[0].append(pltpu.make_async_copy(fluid_in.at[:, z], fp.at[:, 1:rows + 1, z], loc_sem.at[z]))
+        local[0].append(pltpu.make_async_copy(fluid_in.at[:, z], fp.at[:, :, z], loc_sem.at[z]))
         local[1].append(pltpu.make_async_copy(count_in.at[z], cn.at[H:H + R, z], loc_sem.at[NZ + z]))
         local[2].append(pltpu.make_async_copy(drag_in.at[z], dr.at[:, z], loc_sem.at[2 * NZ + z]))
         local[3].append(pltpu.make_async_copy(pvel_in.at[:, z], pv.at[:, :, z], loc_sem.at[3 * NZ + z]))
-    for copies in local:
+    for copy in local[0]:
+        copy.start()
+
+    home = x // C
+    barrier = pltpu.get_barrier_semaphore()
+    for d in range(1, G * K):
+        to = {"gx": lax.rem(x + d // K, G), "gy": lax.rem(k + d % K, K)}
+        pl.semaphore_signal(barrier, inc=1, device_id=to, device_id_type=pl.DeviceIdType.MESH)
+
+    for copies in local[1:]:
         for copy in copies:
             copy.start()
 
-    home = x // C
-    barrier = pltpu.get_barrier_semaphore()
-
-    def greet(to):
-        pl.semaphore_signal(barrier, inc=1, device_id=to, device_id_type=pl.DeviceIdType.MESH)
-
-    for d in range(1, K):
-        greet({"gx": x, "gy": lax.rem(k + d, K)})
-    @pl.when(has_prev)
-    def _():
-        greet(prev_id)
-
-    @pl.when(has_next)
-    def _():
-        greet(next_id)
-
-    for c in range(C):
-        for j in range(K):
-            @pl.when(jnp.logical_or(k * C + c != x, k != j))
-            def _(c=c, j=j):
-                greet({"gx": k * C + c, "gy": jnp.int32(j)})
-
-    for t in range(G):
-        @pl.when(jnp.logical_or(home != k, x != t))
-        def _(t=t):
-            greet({"gx": jnp.int32(t), "gy": home})
-
-    for d in range(1, G):
-        greet({"gx": lax.rem(x + d, G), "gy": k})
-
-    one = jnp.int32(1)
-    nothing = jnp.int32(0)
-    heard = (
-        K - 1 + G - 1 + G + C * K
-        + jnp.where(has_prev, one, nothing)
-        + jnp.where(has_next, one, nothing)
-        - 2 * jnp.where(home == k, one, nothing)
-    )
-
-    @pl.when(k == 0)
-    def _():
-        fp[:, 0:1] = jnp.zeros((3, 1, NZ, W), jnp.float32)
-
-    @pl.when(k == K - 1)
-    def _():
-        fp[:, rows + 1:rows + 2] = jnp.zeros((3, 1, NZ, W), jnp.float32)
-
     line = jnp.zeros((NZ, NY), jnp.float32)
+
+    @pl.when(jnp.logical_not(has_prev))
+    def _():
+        for which in range(3):
+            ub[which, 0] = line
+
+    @pl.when(jnp.logical_not(has_next))
+    def _():
+        for which in range(3):
+            ub[which, R + 1] = line
+
     fl[0] = line
     fl[R + 1] = line
     edge = jnp.zeros((H, NZ, NY), jnp.float32)
@@ -119,65 +92,66 @@
 
     for copy in local[0]:
         copy.wait()
-    pl.semaphore_wait(barrier, heard)
-
-    up = {"gx": x, "gy": lax.rem(k + K - 1, K)}
-    down = {"gx": x, "gy": lax.rem(k + 1, K)}
-    to_up = remote(fp.at[:, 1:2], fp.at[:, rows + 1:rows + 2], fh_send.at[0], fh_recv.at[0], up)
-    to_down = remote(fp.at[:, rows:rows + 1], fp.at[:, 0:1], fh_send.at[1], fh_recv.at[1], down)
-
-    @pl.when(k > 0)
-    def _():
-        to_up.start()
-
-    @pl.when(k < K - 1)
-    def _():
-        to_down.start()
-
-    def part(at):
-        return fp.at[:, pl.ds(at * R, R + 2)]
-
-    def at_edge(c, j):
-        low = (j == 0) if c == 0 else (j < 0)
-        high = (j == K - 1) if c == C - 1 else (j < 0)
-        return jnp.logical_or(low, high)
+    pl.semaphore_wait(barrier, G * K - 1)
 
     columns = pl.ds(pl.multiple_of(x * W, W), W)
-
+    chip = x // C
     sends = []
-    for d in range(K):
-        for c in range(C):
-            j = lax.rem(k + d, K)
-            target = k * C + c
-            src = part(c * K + j)
-            dst = ub.at[:, :, :, columns]
-            far = remote(src, dst, s2_send.at[d * C + c], s2_recv.at[x], {"gx": target, "gy": j})
-            near = pltpu.make_async_copy(src, dst, s2_recv.at[x])
-            sends.append((c, j, far, near, jnp.logical_and(target == x, j == k)))
-
-    def send_all(edges):
-        for c, j, far, near, mine in sends:
-            want = at_edge(c, j) if edges else jnp.logical_not(at_edge(c, j))
-
-            @pl.when(jnp.logical_and(want, mine))
-            def _(near=near):
-                near.start()
-
-            @pl.when(jnp.logical_and(want, jnp.logical_not(mine)))
-            def _(far=far):
-                far.start()
-
-    send_all(False)
-
-    @pl.when(k < K - 1)
-    def _():
-        to_up.wait_recv()
-
-    @pl.when(k > 0)
-    def _():
-        to_down.wait_recv()
-
-    send_all(True)
+    for c in range(C):
+        for d in range(K):
+            j = lax.rem(k + d + K - chip, K)
+            at = (c * K + j) * R
+            mine = jnp.logical_and(k * C + c == x, j == k)
+            low = (j == 0) if c == 0 else None
+            high = (j == K - 1) if c == C - 1 else None
+            inner = jnp.bool_(True)
+            forms = []
+            if low is not None:
+                inner = jnp.logical_and(inner, jnp.logical_not(low))
+                forms.append((low, 0, 1))
+            if high is not None:
+                inner = jnp.logical_and(inner, jnp.logical_not(high))
+                forms.append((high, 1, 0))
+            forms.append((inner, 1, 1))
+            for want, before, after in forms:
+                n = before + R + after
+                src = fp.at[:, pl.ds(at - before, n)]
+                dst = ub.at[:, pl.ds(1 - before, n), :, columns]
+                far = remote(src, dst, s2_send.at[c * K + d], s2_recv.at[x], {"gx": k * C + c, "gy": j})
+                near = pltpu.make_async_copy(src, dst, s2_recv.at[x])
+                near_when = jnp.logical_and(want, mine)
+                far_when = jnp.logical_and(want, jnp.logical_not(mine))
+
+                @pl.when(near_when)
+                def _(near=near):
+                    near.start()
+
+                @pl.when(far_when)
+                def _(far=far):
+                    far.start()
+
+                sends.append((far_when, far))
+
+    for n, (want, row, at, gx, gy) in enumerate((
+        (k > 0, 0, R + 1, jnp.maximum(k * C - 1, 0), K - 1),
+        (k < K - 1, rows - 1, 0, jnp.minimum((k + 1) * C, G - 1), 0),
+    )):
+        src = fp.at[:, row:row + 1]
+        dst = ub.at[:, at:at + 1, :, columns]
+        far = remote(src, dst, row_send.at[n], row_recv.at[x], {"gx": gx, "gy": jnp.int32(gy)})
+        near = pltpu.make_async_copy(src, dst, row_recv.at[x])
+        mine = jnp.logical_and(gx == x, k == gy)
+        far_when = jnp.logical_and(want, jnp.logical_not(mine))
+
+        @pl.when(jnp.logical_and(want, mine))
+        def _(near=near):
+            near.start()
+
+        @pl.when(far_when)
+        def _(far=far):
+            far.start()
+
+        sends.append((far_when, far))
 
     halo_up = [remote(cn.at[H:2 * H], cn.at[H + R:2 * H + R], hal_send.at[0], hal_recv.at[0], prev_id)]
     halo_down = [remote(cn.at[R:R + H], cn.at[0:H], hal_send.at[1], hal_recv.at[1], next_id)]
@@ -254,10 +228,28 @@
         upright = a * pltpu.roll(p, NZ - 1, 0) + pltpu.roll(a * p, 1, 0)
         return (wf[n - 1] * pa + wf[n] * pb) + (across + upright)
 
-    for sender in range(G):
-        spot = pl.ds(sender * W, W)
-        here = {"gx": x, "gy": k}
-        remote(part(0), ub.at[:, :, :, spot], s2_send.at[0], s2_recv.at[sender], here).wait_recv()
+    here = {"gx": x, "gy": k}
+    slab_low = jnp.logical_and(lax.rem(x, C) == 0, k == 0)
+    slab_high = jnp.logical_and(lax.rem(x, C) == C - 1, k == K - 1)
+    at_side = jnp.logical_or(slab_low, slab_high)
+    extra = jnp.logical_or(jnp.logical_and(slab_low, has_prev), jnp.logical_and(slab_high, has_next))
+
+    def landed(n, sem):
+        for sender in range(G):
+            spot = pl.ds(sender * W, W)
+            remote(fp.at[:, 0:n], ub.at[:, 0:n, :, spot], row_send.at[0], sem.at[sender], here).wait_recv()
+
+    @pl.when(at_side)
+    def _():
+        landed(R + 1, s2_recv)
+
+    @pl.when(jnp.logical_not(at_side))
+    def _():
+        landed(R + 2, s2_recv)
+
+    @pl.when(extra)
+    def _():
+        landed(1, row_recv)
 
     def pass_on(src_up, dst_up, src_down, dst_down, ssem, rsem, at):
         return (
@@ -440,18 +432,10 @@
     for copy in written:
         copy.start()
 
-    @pl.when(k > 0)
-    def _():
-        to_up.wait_send()
-
-    @pl.when(k < K - 1)
-    def _():
-        to_down.wait_send()
-
-    for c, j, far, near, mine in sends:
-        @pl.when(jnp.logical_not(mine))
-        def _(far=far):
-            far.wait_send()
+    for want, copy in sends:
+        @pl.when(want)
+        def _(copy=copy):
+            copy.wait_send()
 
     @pl.when(has_prev)
     def _():
@@ -463,7 +447,6 @@
         for copy in halo_down:
             copy.wait_send()
 
-    here = {"gx": x, "gy": k}
     rises = []
     for d in range(K):
         to = lax.rem(home + d, K)
@@ -523,7 +506,7 @@
     dma = pltpu.SemaphoreType.DMA
     pad = (R + 2 * H, NZ, NY)
     scratch = [
-        pltpu.VMEM((3, rows + 2, NZ, W), f32),
+        pltpu.VMEM((3, rows, NZ, W), f32),
         pltpu.VMEM((3, R + 2, NZ, NY), f32),
         pltpu.VMEM(pad, jnp.int32),
         pltpu.VMEM((R, NZ, NY), f32),
@@ -537,7 +520,7 @@
         pltpu.VMEM((SWEEPS,) + pad, f32),
         pltpu.VMEM((G, R, NZ, W), f32),
         pltpu.VMEM((C, K, R, NZ, W), f32),
-        dma((4 * NZ,)), dma((2,)), dma((2,)),
+        dma((4 * NZ,)), dma((2,)), dma((G,)),
         dma((K * C,)), dma((G,)),
         dma((2,)), dma((2,)), dma((2, H + 1)), dma((2, H + 1)), dma((2, H)), dma((2, H)), dma((G,)), dma((G,)), dma((K,)), dma((K,)),
     ]

time: 70.4 us -> 64.7 us (0.919)
  Pallas kernels: 68.6 us -> 63 us
    pallas_call x1, Pallas kernels: 65.9 us -> 60.3 us  [shards(): pl.pallas_call(functools.partial(kernel, K, G, R, NZ, NY, W), out_shape=(...]
where the time goes in v3:
time: 64.7 us; the launch traced here: 63.6 us
  Pallas kernels  63 us (97%)
    pallas_call x1, Pallas kernels, shards(): pl.pallas_call(functools.partial(kernel, K, G, R, NZ, NY, W), out_shape=(...  60.3 us
    pallas_call x1, Pallas kernels, shards(): pl.pallas_call(settle, out_shape=[jax.ShapeDtypeStruct(v.shape, f32) for...  2.7 us

profile of v3, /device:TPU:0, one launch (start us, length us, event | category | flops | bytes accessed | tf_op | source)
XLA Modules:
  0.0 63.6 jit_solution(4916974154317223776)
XLA Ops:
  0.6 60.3 %shard_map.67 = (f32[8,2,4,8,128]{4,3,2,1,0:T(8,128)}, f32[3,8,8,1024]{3,2,1,0:T(8,128)}, f32[3,8,8,1024]{3,2,1,0:T(8,128)}) custom-call(s32[8,8,1024]{2,1,0:T(8,128)} %count_in.1, f32[8,8,1024]{2,1,0:T(8,128)} %drag_in.1, f32[3,8,8,1024]{3,2,1,0:T(8,128)} %pvel_in.1, f32[3,8,64,128]{3,2,1,0:T(8,128)} %fluid_in.1), custom_call_target="tpu_custom_call" | custom-call | tf_op jit(solution)/shard_map/pallas_call | solution.py:528
  60.9 2.7 %shard_map.68 = (f32[8,64,128]{2,1,0:T(8,128)}, f32[3,8,8,1024]{3,2,1,0:T(8,128)}, f32[3,8,8,1024]{3,2,1,0:T(8,128)}) custom-call(f32[8,64,128]{2,1,0:T(8,128)} %bitcast.1, f32[3,8,8,1024]{3,2,1,0:T(8,128)} %get-tuple-element.7.refs_1_, f32[3,8,8,1024]{3,2,1,0:T(8,128)} %get-tuple-element.8.refs_2_), custom_call_target="tpu_custom_call" | custom-call | tf_op jit(solution)/shard_map/pallas_call | solution.py:541

commit v4 on v3

--- a/solution.py
+++ b/solution.py
@@ -19,7 +19,7 @@
     K, G, R, NZ, NY, W,
     count_in, drag_in, pvel_in, fluid_in,
     press_out, vel_out, grad_out,
-    fp, ub, cn, dr, pv, vo, total_w, wf, wr, wa, rh, pred, gr, fl, fr, eb, lv, rl, po,
+    fp, ub, cn, dr, pv, vo, total_w, wf, wr, wa, rh, pred, gr, fl, fr, eb, lv, rl,
     loc_sem, row_send, row_recv, s2_send, s2_recv,
     hal_send, hal_recv, b_send, b_recv, p_send, p_recv, out_send, out_recv, up_send, up_recv,
 ):
@@ -49,16 +49,13 @@
         local[1].append(pltpu.make_async_copy(count_in.at[z], cn.at[H:H + R, z], loc_sem.at[NZ + z]))
         local[2].append(pltpu.make_async_copy(drag_in.at[z], dr.at[:, z], loc_sem.at[2 * NZ + z]))
         local[3].append(pltpu.make_async_copy(pvel_in.at[:, z], pv.at[:, :, z], loc_sem.at[3 * NZ + z]))
-    for copy in local[0]:
-        copy.start()
-
     home = x // C
     barrier = pltpu.get_barrier_semaphore()
     for d in range(1, G * K):
         to = {"gx": lax.rem(x + d // K, G), "gy": lax.rem(k + d % K, K)}
         pl.semaphore_signal(barrier, inc=1, device_id=to, device_id_type=pl.DeviceIdType.MESH)
 
-    for copies in local[1:]:
+    for copies in local:
         for copy in copies:
             copy.start()
 
@@ -93,6 +90,52 @@
     for copy in local[0]:
         copy.wait()
     pl.semaphore_wait(barrier, G * K - 1)
+
+    def count_rows(begin, stop, at):
+        return (
+            remote(cn.at[H + begin:H + stop], cn.at[H + R + begin:H + R + stop], hal_send.at[at, 0], hal_recv.at[at, 0], prev_id),
+            remote(cn.at[H + R - stop:H + R - begin], cn.at[H - stop:H - begin], hal_send.at[at, 1], hal_recv.at[at, 1], next_id),
+        )
+
+    near_counts, far_counts = count_rows(0, 1, 0), count_rows(1, H, 1)
+
+    turned = k == K - 1
+
+    def launch(copies):
+        @pl.when(jnp.logical_and(turned, has_next))
+        def _():
+            copies[1].start()
+
+        @pl.when(has_prev)
+        def _():
+            copies[0].start()
+
+        @pl.when(jnp.logical_and(jnp.logical_not(turned), has_next))
+        def _():
+            copies[1].start()
+
+    def arrived(copies):
+        @pl.when(has_next)
+        def _():
+            copies[0].wait_recv()
+
+        @pl.when(has_prev)
+        def _():
+            copies[1].wait_recv()
+
+    def sent(copies):
+        @pl.when(has_prev)
+        def _():
+            copies[0].wait_send()
+
+        @pl.when(has_next)
+        def _():
+            copies[1].wait_send()
+
+    for copy in local[1]:
+        copy.wait()
+
+    launch(near_counts)
 
     columns = pl.ds(pl.multiple_of(x * W, W), W)
     chip = x // C
@@ -153,32 +196,11 @@
 
         sends.append((far_when, far))
 
-    halo_up = [remote(cn.at[H:2 * H], cn.at[H + R:2 * H + R], hal_send.at[0], hal_recv.at[0], prev_id)]
-    halo_down = [remote(cn.at[R:R + H], cn.at[0:H], hal_send.at[1], hal_recv.at[1], next_id)]
-
-    for copies in local[1:]:
+    launch(far_counts)
+    arrived(near_counts)
+    for copies in local[2:]:
         for copy in copies:
             copy.wait()
-
-    @pl.when(has_prev)
-    def _():
-        for copy in halo_up:
-            copy.start()
-
-    @pl.when(has_next)
-    def _():
-        for copy in halo_down:
-            copy.start()
-
-    @pl.when(has_next)
-    def _():
-        for copy in halo_up:
-            copy.wait_recv()
-
-    @pl.when(has_prev)
-    def _():
-        for copy in halo_down:
-            copy.wait_recv()
 
     lane = lax.broadcasted_iota(jnp.int32, (NZ, NY), 1)
     level = lax.broadcasted_iota(jnp.int32, (NZ, NY), 0)
@@ -207,7 +229,7 @@
         vo[n] = jnp.where(inside(n - H), v, 0.0)
         return carry
 
-    lax.fori_loop(0, R + 2 * H, voids_row, 0)
+    lax.fori_loop(H - 1, R + H + 1, voids_row, 0)
 
     def weight_row(n, carry):
         v = vo[n]
@@ -219,8 +241,8 @@
         wa[n] = jnp.where(level < NZ - 1, 0.5 * (v + pltpu.roll(v, NZ - 1, 0)), 0.0)
         return carry
 
-    wf[0] = 0.5 * (vo[0] + vo[1])
-    lax.fori_loop(1, R + 2 * H - 1, weight_row, 0)
+    wf[H - 1] = 0.5 * (vo[H - 1] + vo[H])
+    lax.fori_loop(H, R + H, weight_row, 0)
 
     def weighted(n, p, pa, pb):
         r, a = wr[n], wa[n]
@@ -228,6 +250,12 @@
         upright = a * pltpu.roll(p, NZ - 1, 0) + pltpu.roll(a * p, 1, 0)
         return (wf[n - 1] * pa + wf[n] * pb) + (across + upright)
 
+    for want, copy in sends:
+        @pl.when(want)
+        def _(copy=copy):
+            copy.wait_send()
+
+
     here = {"gx": x, "gy": k}
     slab_low = jnp.logical_and(lax.rem(x, C) == 0, k == 0)
     slab_high = jnp.logical_and(lax.rem(x, C) == C - 1, k == K - 1)
@@ -271,33 +299,6 @@
 
     def mid_rows(s):
         return level_rows(lv.at[first], s, p_send, p_recv, s)
-
-    def launch(copies):
-        @pl.when(has_prev)
-        def _():
-            copies[0].start()
-
-        @pl.when(has_next)
-        def _():
-            copies[1].start()
-
-    def arrived(copies):
-        @pl.when(has_next)
-        def _():
-            copies[0].wait_recv()
-
-        @pl.when(has_prev)
-        def _():
-            copies[1].wait_recv()
-
-    def sent(copies):
-        @pl.when(has_prev)
-        def _():
-            copies[0].wait_send()
-
-        @pl.when(has_next)
-        def _():
-            copies[1].wait_send()
 
     def momentum(i, which):
         v, ws, drag, u = vo[H + i], total_w[H + i], dr[i], ub[which, i + 1]
@@ -352,6 +353,13 @@
     finish(R - half)
     if half <= H:
         launch(base_rows(half - 1))
+
+    arrived(far_counts)
+    lax.fori_loop(0, H - 1, voids_row, 0)
+    lax.fori_loop(R + H + 1, R + 2 * H, voids_row, 0)
+    wf[0] = 0.5 * (vo[0] + vo[1])
+    lax.fori_loop(1, H, weight_row, 0)
+    lax.fori_loop(R + H, R + 2 * H - 1, weight_row, 0)
 
     def sweep_pair(l, lo):
         hi = 2 * H + R - 1 - lo
@@ -401,15 +409,45 @@
         low = l - last_level - 1 + (1 if l in (first + 1, last_level) else 0)
         rows_of(l, low, l - H)
 
+    def partner(d, back=False):
+        if K & (K - 1) == 0:
+            return chip ^ d
+        return lax.rem(chip + (K - d if back else d), K)
+
     outs = []
-    for e in range(1, G):
-        target = lax.rem(x + e, G)
-        src = pf.at[H:H + R, :, pl.ds(pl.multiple_of(target * W, W), W)]
-        outs.append(remote(src, rl.at[x], out_send.at[e], out_recv.at[x], {"gx": target, "gy": k}))
-    kept = pltpu.make_async_copy(pf.at[H:H + R, :, columns], rl.at[x], out_recv.at[x])
-    kept.start()
-    for copy in outs:
-        copy.start()
+    for d in range(K):
+        for c in range(C):
+            target = partner(d) * C + lax.rem(x + c, C)
+            src = pf.at[H:H + R, :, pl.ds(pl.multiple_of(target * W, W), W)]
+            if d == c == 0:
+                pltpu.make_async_copy(src, rl.at[x], out_recv.at[x]).start()
+            else:
+                outs.append(remote(src, rl.at[x], out_send.at[d * C + c], out_recv.at[x], {"gx": target, "gy": k}))
+                outs[-1].start()
+
+    rises = []
+
+    def rise(d):
+        to = partner(d, back=True)
+        for c in range(C):
+            slot = to * C + c
+            remote(pf.at[H:H + R, :, 0:W], rl.at[slot], out_send.at[0], out_recv.at[slot], here).wait_recv()
+        src = rl.at[pl.ds(to * C, C)]
+        far = remote(src, press_out.at[:, k], up_send.at[d], up_recv.at[k], {"gx": x, "gy": to})
+        near = pltpu.make_async_copy(src, press_out.at[:, k], up_recv.at[k])
+
+        @pl.when(to != k)
+        def _():
+            far.start()
+
+        @pl.when(to == k)
+        def _():
+            near.start()
+
+        rises.append((to, far))
+
+    for d in range(K):
+        rise(d)
 
     rows_of(last_level, -1, 0)
 
@@ -432,42 +470,7 @@
     for copy in written:
         copy.start()
 
-    for want, copy in sends:
-        @pl.when(want)
-        def _(copy=copy):
-            copy.wait_send()
-
-    @pl.when(has_prev)
-    def _():
-        for copy in halo_up:
-            copy.wait_send()
-
-    @pl.when(has_next)
-    def _():
-        for copy in halo_down:
-            copy.wait_send()
-
-    rises = []
-    for d in range(K):
-        to = lax.rem(home + d, K)
-        for c in range(C):
-            slot = to * C + c
-            remote(pf.at[H:H + R, :, 0:W], rl.at[slot], out_send.at[0], out_recv.at[slot], here).wait_recv()
-        src = rl.at[pl.ds(to * C, C)]
-        far = remote(src, po.at[:, k], up_send.at[d], up_recv.at[k], {"gx": x, "gy": to})
-        near = pltpu.make_async_copy(src, po.at[:, k], up_recv.at[k])
-
-        @pl.when(to != k)
-        def _(far=far):
-            far.start()
-
-        @pl.when(to == k)
-        def _(near=near):
-            near.start()
-
-        rises.append((to, far))
-
-    for copies in [flux_rows(), edge_rows()] + [base_rows(i) for i in range(1, H)] + [mid_rows(i) for i in range(first)]:
+    for copies in [near_counts, far_counts, flux_rows(), edge_rows()] + [base_rows(i) for i in range(1, H)] + [mid_rows(i) for i in range(first)]:
         sent(copies)
 
     for copy in outs:
@@ -479,21 +482,35 @@
             far.wait_send()
 
     for j in range(K):
-        remote(rl.at[0:C], po.at[:, j], up_send.at[0], up_recv.at[j], here).wait_recv()
-    last = [pltpu.make_async_copy(po.at[:, :, :, z], press_out.at[z], loc_sem.at[2 * NZ + z]) for z in range(NZ)]
-    for copy in last:
-        copy.start()
-    for copy in written + last:
+        remote(rl.at[0:C], press_out.at[:, j], up_send.at[0], up_recv.at[j], here).wait_recv()
+    for copy in written:
         copy.wait()
 
 
-def settle(*refs):
-    n = len(refs) // 2
-    copies = [pltpu.make_async_copy(refs[i], refs[n + i], refs[-1].at[i]) for i in range(n)]
-    for copy in copies:
-        copy.start()
-    for copy in copies:
-        copy.wait()
+def settle(press_in, vel_in, grad_in, press_out, vel_out, grad_out, press, vel, grad, in_sem, out_sem):
+    C, K, R, NZ, W = press.shape
+    steps = []
+
+    def step(src, held, stores):
+        at = len(steps)
+        steps.append((pltpu.make_async_copy(src, held, in_sem.at[at]), stores))
+
+    step(press_in, press, [pltpu.make_async_copy(press.at[:, :, :, z], press_out.at[z], out_sem.at[2 * vel.shape[0] + z]) for z in range(NZ)])
+
+    for n, (src, held, dst) in enumerate(((vel_in, vel, vel_out), (grad_in, grad, grad_out))):
+        for i in range(held.shape[0]):
+            stores = [pltpu.make_async_copy(held.at[i], dst.at[i], out_sem.at[n * held.shape[0] + i])]
+            step(src.at[i], held.at[i], stores)
+
+    for load, _ in steps:
+        load.start()
+    for load, stores in steps:
+        load.wait()
+        for store in stores:
+            store.start()
+    for _, stores in steps:
+        for store in stores:
+            store.wait()
 
 
 def shards(K, G, particle_count, drag_coeff, particle_velocity, fluid_velocity):
@@ -519,16 +536,15 @@
         pltpu.VMEM((2, NZ, NY), f32),
         pltpu.VMEM((SWEEPS,) + pad, f32),
         pltpu.VMEM((G, R, NZ, W), f32),
-        pltpu.VMEM((C, K, R, NZ, W), f32),
         dma((4 * NZ,)), dma((2,)), dma((G,)),
         dma((K * C,)), dma((G,)),
-        dma((2,)), dma((2,)), dma((2, H + 1)), dma((2, H + 1)), dma((2, H)), dma((2, H)), dma((G,)), dma((G,)), dma((K,)), dma((K,)),
+        dma((2, 2)), dma((2, 2)), dma((2, H + 1)), dma((2, H + 1)), dma((2, H)), dma((2, H)), dma((G,)), dma((G,)), dma((K,)), dma((K,)),
     ]
     anywhere = pl.BlockSpec(memory_space=pl.ANY)
     pressure, velocity, slopes = pl.pallas_call(
         functools.partial(kernel, K, G, R, NZ, NY, W),
         out_shape=(
-            jax.ShapeDtypeStruct((NZ, C, K, R, W), f32),
+            jax.ShapeDtypeStruct((C, K, R, NZ, W), f32),
             jax.ShapeDtypeStruct((3, NZ, R, NY), f32),
             jax.ShapeDtypeStruct((3, NZ, R, NY), f32),
         ),
@@ -537,14 +553,20 @@
         scratch_shapes=scratch,
         compiler_params=pltpu.CompilerParams(collective_id=0, has_side_effects=True, vmem_limit_bytes=67043328),
     )(particle_count, drag_coeff, particle_velocity, fluid_velocity)
-    found = (pressure.reshape(NZ, rows, W), velocity, slopes)
-    return pl.pallas_call(
+    first = [pressure, velocity, slopes]
+    pressure, velocity, slopes = pl.pallas_call(
         settle,
-        out_shape=[jax.ShapeDtypeStruct(v.shape, f32) for v in found],
-        in_specs=[pl.BlockSpec(memory_space=pltpu.VMEM)] * 3,
+        out_shape=[
+            jax.ShapeDtypeStruct((NZ, C, K, R, W), f32),
+            jax.ShapeDtypeStruct(velocity.shape, f32),
+            jax.ShapeDtypeStruct(slopes.shape, f32),
+        ],
+        in_specs=[anywhere] * 3,
         out_specs=[anywhere] * 3,
-        scratch_shapes=[dma((3,))],
-    )(*found)
+        scratch_shapes=[*[pltpu.VMEM(v.shape, f32) for v in first], dma((1 + 2 * 3,)), dma((NZ + 2 * 3,))],
+        compiler_params=pltpu.CompilerParams(vmem_limit_bytes=67043328),
+    )(*first)
+    return pressure.reshape(NZ, rows, W), velocity, slopes
 
 
 def solution(mesh):

time: 64.7 us -> 62.9 us (0.972); the launches traced: 63.6 us -> 62.7 us
  Pallas kernels: 63 us -> 62.1 us
where the time goes in v4:
time: 62.9 us; the launch traced here: 62.7 us
  Pallas kernels  62.1 us (99%)
  between operations  0.64 us (1%)
    pallas_call x1, Pallas kernels, shards(): pl.pallas_call(functools.partial(kernel, K, G, R, NZ, NY, W), out_shape=(...  59.7 us
    pallas_call x1, Pallas kernels, shards(): pl.pallas_call(settle, out_shape=[jax.ShapeDtypeStruct((NZ, C, K, R, W),...  2.35 us

profile of v4, /device:TPU:0, one launch (start us, length us, event | category | flops | bytes accessed | tf_op | source)
XLA Modules:
  0.0 62.7 jit_solution(3782376138822429024)
XLA Ops:
  0.6 59.7 %shard_map.67 = (f32[2,4,8,8,128]{4,3,2,1,0:T(8,128)}, f32[3,8,8,1024]{3,2,1,0:T(8,128)}, f32[3,8,8,1024]{3,2,1,0:T(8,128)}) custom-call(s32[8,8,1024]{2,1,0:T(8,128)} %count_in.1, f32[8,8,1024]{2,1,0:T(8,128)} %drag_in.1, f32[3,8,8,1024]{3,2,1,0:T(8,128)} %pvel_in.1, f32[3,8,64,128]{3,2,1,0:T(8,128)} %fluid_in.1), custom_call_target="tpu_custom_call" | custom-call | tf_op jit(solution)/shard_map/pallas_call | solution.py:544
  60.3 2.4 %shard_map.68 = (f32[8,2,4,8,128]{4,3,2,1,0:T(8,128)}, f32[3,8,8,1024]{3,2,1,0:T(8,128)}, f32[3,8,8,1024]{3,2,1,0:T(8,128)}) custom-call(f32[2,4,8,8,128]{4,3,2,1,0:T(8,128)} %get-tuple-element.9.press_in, f32[3,8,8,1024]{3,2,1,0:T(8,128)} %get-tuple-element.10.vel_in, f32[3,8,8,1024]{3,2,1,0:T(8,128)} %get-tuple-element.11.grad_in), custom_call_target="tpu_custom_call" | custom-call | tf_op jit(solution)/shard_map/pallas_call | solution.py:557

commit v5 on v4

--- a/solution.py
+++ b/solution.py
@@ -78,14 +78,16 @@
     @pl.when(jnp.logical_not(has_prev))
     def _():
         fr[0] = line
-        lv[0, 0:H] = edge
-        lv[first, 0:H] = edge
+        for l in (0, first):
+            lv[l, 0:H] = edge
+            lv[l + 1, 1] = line
 
     @pl.when(jnp.logical_not(has_next))
     def _():
         fr[1] = line
-        lv[0, H + R:2 * H + R] = edge
-        lv[first, H + R:2 * H + R] = edge
+        for l in (0, first):
+            lv[l, H + R:2 * H + R] = edge
+            lv[l + 1, 2 * H + R - 2] = line
 
     for copy in local[0]:
         copy.wait()
@@ -97,22 +99,18 @@
             remote(cn.at[H + R - stop:H + R - begin], cn.at[H - stop:H - begin], hal_send.at[at, 1], hal_recv.at[at, 1], next_id),
         )
 
-    near_counts, far_counts = count_rows(0, 1, 0), count_rows(1, H, 1)
+    near_counts, far_counts = count_rows(0, 1, 0), count_rows(1, H - 1, 1)
 
     turned = k == K - 1
-
-    def launch(copies):
-        @pl.when(jnp.logical_and(turned, has_next))
-        def _():
-            copies[1].start()
-
-        @pl.when(has_prev)
-        def _():
-            copies[0].start()
-
-        @pl.when(jnp.logical_and(jnp.logical_not(turned), has_next))
-        def _():
-            copies[1].start()
+    wraps = (jnp.logical_and(k == 0, has_prev), jnp.logical_and(turned, has_next))
+    plain = (jnp.logical_and(k > 0, has_prev), jnp.logical_and(jnp.logical_not(turned), has_next))
+
+    def launch(copies, only=None):
+        for group in ((wraps, plain) if only is None else (only,)):
+            for when, copy in zip(group, copies):
+                @pl.when(when)
+                def _(copy=copy):
+                    copy.start()
 
     def arrived(copies):
         @pl.when(has_next)
@@ -294,11 +292,17 @@
     def base_rows(s):
         return level_rows(b, s, b_send, b_recv, s + 1)
 
+    def base_last():
+        return level_rows(lv.at[1], H - 2, b_send, b_recv, H)
+
     def edge_rows():
         return pass_on(eb.at[0], b.at[H + R], eb.at[1], b.at[H - 1], b_send, b_recv, 1)
 
     def mid_rows(s):
         return level_rows(lv.at[first], s, p_send, p_recv, s)
+
+    def mid_last():
+        return level_rows(lv.at[first + 1], H - 2, p_send, p_recv, H - 1)
 
     def momentum(i, which):
         v, ws, drag, u = vo[H + i], total_w[H + i], dr[i], ub[which, i + 1]
@@ -341,7 +345,7 @@
                 eb[1] = b[H + R - 1]
                 launch(edge_rows())
 
-            @pl.when(jnp.logical_and(s > 1, s <= H))
+            @pl.when(jnp.logical_and(s > 1, s < H))
             def _():
                 launch(base_rows(s - 1))
 
@@ -351,15 +355,6 @@
     lax.fori_loop(0, half, momentum_step, 0)
     finish(half - 1)
     finish(R - half)
-    if half <= H:
-        launch(base_rows(half - 1))
-
-    arrived(far_counts)
-    lax.fori_loop(0, H - 1, voids_row, 0)
-    lax.fori_loop(R + H + 1, R + 2 * H, voids_row, 0)
-    wf[0] = 0.5 * (vo[0] + vo[1])
-    lax.fori_loop(1, H, weight_row, 0)
-    lax.fori_loop(R + H, R + 2 * H - 1, weight_row, 0)
 
     def sweep_pair(l, lo):
         hi = 2 * H + R - 1 - lo
@@ -385,25 +380,36 @@
 
     for j in range(2 - half, H + 1):
         if j == 0:
+            arrived(far_counts)
+            lax.fori_loop(1, H - 1, voids_row, 0)
+            lax.fori_loop(R + H + 1, R + 2 * H - 1, voids_row, 0)
+            wf[1] = 0.5 * (vo[1] + vo[2])
+            lax.fori_loop(2, H, weight_row, 0)
+            lax.fori_loop(R + H, R + 2 * H - 2, weight_row, 0)
             arrived(flux_rows())
             b[H] = b[H] + fr[0] * rh[H]
             b[H + R - 1] = b[H + R - 1] - fr[1] * rh[H + R - 1]
+        elif j == H:
+            arrived(base_last())
         elif j > 0:
             arrived(base_rows(j - 1))
             if j == 1:
                 b[H - 1] = b[H - 1] - fl[1] * rh[H - 1]
                 b[H + R] = b[H + R] + fl[R] * rh[H + R]
         stop = min(last_level, j + half - 1) + 1
-        diagonal(j, 1, min(stop, first + 1))
-        if j > 0:
+        diagonal(j, 2 if j == H else 1, min(stop, first + 1))
+        if j == 3 - H:
+            launch(base_last())
+        if j > 1:
             launch(mid_rows(first - j))
         if stop > first + 1:
             diagonal(j, first + 1, stop)
-
-    depth = last_level - first
-    for s in range(first - 1, 0, -1):
+        if j == first + 3 - H:
+            launch(mid_last())
+
+    for s in range(first - 2, 0, -1):
         arrived(mid_rows(s))
-    rows_of(first + 1, -depth, 1 - depth)
+    arrived(mid_last())
     arrived(mid_rows(0))
     for l in range(first + 1, last_level + 1):
         low = l - last_level - 1 + (1 if l in (first + 1, last_level) else 0)
@@ -470,7 +476,7 @@
     for copy in written:
         copy.start()
 
-    for copies in [near_counts, far_counts, flux_rows(), edge_rows()] + [base_rows(i) for i in range(1, H)] + [mid_rows(i) for i in range(first)]:
+    for copies in [near_counts, far_counts, flux_rows(), edge_rows()] + [base_rows(i) for i in range(1, H - 1)] + [base_last(), mid_last()] + [mid_rows(i) for i in range(first - 1)]:
         sent(copies)
 
     for copy in outs:

time: 62.9 us -> 62.6 us (level)
  no operation moved by 1% of the time
where the time goes in v5:
time: 62.6 us; the launch traced here: 62.4 us
  Pallas kernels  61.8 us (99%)
  between operations  0.64 us (1%)
    pallas_call x1, Pallas kernels, shards(): pl.pallas_call(functools.partial(kernel, K, G, R, NZ, NY, W), out_shape=(...  59.4 us
    pallas_call x1, Pallas kernels, shards(): pl.pallas_call(settle, out_shape=[jax.ShapeDtypeStruct((NZ, C, K, R, W),...  2.35 us

profile of v5, /device:TPU:0, one launch (start us, length us, event | category | flops | bytes accessed | tf_op | source)
XLA Modules:
  0.0 62.4 jit_solution(708520706925204319)
XLA Ops:
  0.6 59.4 %shard_map.67 = (f32[2,4,8,8,128]{4,3,2,1,0:T(8,128)}, f32[3,8,8,1024]{3,2,1,0:T(8,128)}, f32[3,8,8,1024]{3,2,1,0:T(8,128)}) custom-call(s32[8,8,1024]{2,1,0:T(8,128)} %count_in.1, f32[8,8,1024]{2,1,0:T(8,128)} %drag_in.1, f32[3,8,8,1024]{3,2,1,0:T(8,128)} %pvel_in.1, f32[3,8,64,128]{3,2,1,0:T(8,128)} %fluid_in.1), custom_call_target="tpu_custom_call" | custom-call | tf_op jit(solution)/shard_map/pallas_call | solution.py:550
  60.1 2.4 %shard_map.68 = (f32[8,2,4,8,128]{4,3,2,1,0:T(8,128)}, f32[3,8,8,1024]{3,2,1,0:T(8,128)}, f32[3,8,8,1024]{3,2,1,0:T(8,128)}) custom-call(f32[2,4,8,8,128]{4,3,2,1,0:T(8,128)} %get-tuple-element.9.press_in, f32[3,8,8,1024]{3,2,1,0:T(8,128)} %get-tuple-element.10.vel_in, f32[3,8,8,1024]{3,2,1,0:T(8,128)} %get-tuple-element.11.grad_in), custom_call_target="tpu_custom_call" | custom-call | tf_op jit(solution)/shard_map/pallas_call | solution.py:563

commit v6 on v5

--- a/solution.py
+++ b/solution.py
@@ -140,7 +140,7 @@
     sends = []
     for c in range(C):
         for d in range(K):
-            j = lax.rem(k + d + K - chip, K)
+            j = k ^ d ^ chip if K & (K - 1) == 0 else lax.rem(k + d + K - chip, K)
             at = (c * K + j) * R
             mine = jnp.logical_and(k * C + c == x, j == k)
             low = (j == 0) if c == 0 else None
@@ -376,7 +376,7 @@
             sweep_pair(l, lo)
             return carry
 
-        lax.fori_loop(H + start, H + stop, row, 0)
+        lax.fori_loop(H + start, H + stop, row, 0, unroll=True)
 
     for j in range(2 - half, H + 1):
         if j == 0:

time: 62.6 us -> 61.3 us (0.979)
  the two profiles are of different devices: /device:TPU:0 before, /device:TPU:6 now
where the time goes in v6:
time: 61.3 us; the launch traced here: 61.1 us
  Pallas kernels  60.4 us (99%)
  between operations  0.64 us (1%)
    pallas_call x1, Pallas kernels, shards(): pl.pallas_call(functools.partial(kernel, K, G, R, NZ, NY, W), out_shape=(...  58.1 us
    pallas_call x1, Pallas kernels, shards(): pl.pallas_call(settle, out_shape=[jax.ShapeDtypeStruct((NZ, C, K, R, W),...  2.35 us

profile of v6, /device:TPU:6, one launch (start us, length us, event | category | flops | bytes accessed | tf_op | source)
XLA Modules:
  0.0 61.1 jit_solution(11910490837554603062)
XLA Ops:
  0.6 58.1 %shard_map.67 = (f32[2,4,8,8,128]{4,3,2,1,0:T(8,128)}, f32[3,8,8,1024]{3,2,1,0:T(8,128)}, f32[3,8,8,1024]{3,2,1,0:T(8,128)}) custom-call(s32[8,8,1024]{2,1,0:T(8,128)} %count_in.1, f32[8,8,1024]{2,1,0:T(8,128)} %drag_in.1, f32[3,8,8,1024]{3,2,1,0:T(8,128)} %pvel_in.1, f32[3,8,64,128]{3,2,1,0:T(8,128)} %fluid_in.1), custom_call_target="tpu_custom_call" | custom-call | tf_op jit(solution)/shard_map/pallas_call | solution.py:550
  58.7 2.4 %shard_map.68 = (f32[8,2,4,8,128]{4,3,2,1,0:T(8,128)}, f32[3,8,8,1024]{3,2,1,0:T(8,128)}, f32[3,8,8,1024]{3,2,1,0:T(8,128)}) custom-call(f32[2,4,8,8,128]{4,3,2,1,0:T(8,128)} %get-tuple-element.9.press_in, f32[3,8,8,1024]{3,2,1,0:T(8,128)} %get-tuple-element.10.vel_in, f32[3,8,8,1024]{3,2,1,0:T(8,128)} %get-tuple-element.11.grad_in), custom_call_target="tpu_custom_call" | custom-call | tf_op jit(solution)/shard_map/pallas_call | solution.py:563

commit v7 on v6

--- a/solution.py
+++ b/solution.py
@@ -8,7 +8,7 @@
 from jax.sharding import PartitionSpec as P
 
 SWEEPS = 8
-ROUNDS = (4, 4)
+ROUNDS = (4, 3)
 
 particle_volume = 0.05
 time_step = 0.5
@@ -78,16 +78,18 @@
     @pl.when(jnp.logical_not(has_prev))
     def _():
         fr[0] = line
-        for l in (0, first):
-            lv[l, 0:H] = edge
-            lv[l + 1, 1] = line
+        lv[0, 0:H] = edge
+        lv[1, 1] = line
+        lv[first, 0:H] = edge
+        lv[last_level, H - 1] = line
 
     @pl.when(jnp.logical_not(has_next))
     def _():
         fr[1] = line
-        for l in (0, first):
-            lv[l, H + R:2 * H + R] = edge
-            lv[l + 1, 2 * H + R - 2] = line
+        lv[0, H + R:2 * H + R] = edge
+        lv[1, 2 * H + R - 2] = line
+        lv[first, H + R:2 * H + R] = edge
+        lv[last_level, H + R] = line
 
     for copy in local[0]:
         copy.wait()
@@ -301,8 +303,8 @@
     def mid_rows(s):
         return level_rows(lv.at[first], s, p_send, p_recv, s)
 
-    def mid_last():
-        return level_rows(lv.at[first + 1], H - 2, p_send, p_recv, H - 1)
+    def last_rows():
+        return level_rows(pf, 0, p_send, p_recv, H - 1)
 
     def momentum(i, which):
         v, ws, drag, u = vo[H + i], total_w[H + i], dr[i], ub[which, i + 1]
@@ -400,20 +402,15 @@
         diagonal(j, 2 if j == H else 1, min(stop, first + 1))
         if j == 3 - H:
             launch(base_last())
-        if j > 1:
+        if first - j < ROUNDS[1]:
             launch(mid_rows(first - j))
         if stop > first + 1:
             diagonal(j, first + 1, stop)
-        if j == first + 3 - H:
-            launch(mid_last())
-
-    for s in range(first - 2, 0, -1):
+
+    for s in range(ROUNDS[1] - 1, -1, -1):
         arrived(mid_rows(s))
-    arrived(mid_last())
-    arrived(mid_rows(0))
     for l in range(first + 1, last_level + 1):
-        low = l - last_level - 1 + (1 if l in (first + 1, last_level) else 0)
-        rows_of(l, low, l - H)
+        rows_of(l, l - last_level, l - H)
 
     def partner(d, back=False):
         if K & (K - 1) == 0:
@@ -431,6 +428,7 @@
                 outs.append(remote(src, rl.at[x], out_send.at[d * C + c], out_recv.at[x], {"gx": target, "gy": k}))
                 outs[-1].start()
 
+    launch(last_rows())
     rises = []
 
     def rise(d):
@@ -455,7 +453,7 @@
     for d in range(K):
         rise(d)
 
-    rows_of(last_level, -1, 0)
+    arrived(last_rows())
 
     def slope_row(i, carry):
         n = H + i
@@ -476,7 +474,7 @@
     for copy in written:
         copy.start()
 
-    for copies in [near_counts, far_counts, flux_rows(), edge_rows()] + [base_rows(i) for i in range(1, H - 1)] + [base_last(), mid_last()] + [mid_rows(i) for i in range(first - 1)]:
+    for copies in [near_counts, far_counts, flux_rows(), edge_rows()] + [base_rows(i) for i in range(1, H - 1)] + [base_last(), last_rows()] + [mid_rows(i) for i in range(ROUNDS[1])]:
         sent(copies)
 
     for copy in outs:

time: 61.3 us -> 59.6 us (0.972)
  the two profiles are of different devices: /device:TPU:6 before, /device:TPU:0 now
where the time goes in v7:
time: 59.6 us; the launch traced here: 58.8 us
  Pallas kernels  58.2 us (98%)
  between operations  0.64 us (1%)
    pallas_call x1, Pallas kernels, shards(): pl.pallas_call(functools.partial(kernel, K, G, R, NZ, NY, W), out_shape=(...  55.8 us
    pallas_call x1, Pallas kernels, shards(): pl.pallas_call(settle, out_shape=[jax.ShapeDtypeStruct((NZ, C, K, R, W),...  2.35 us

profile of v7, /device:TPU:0, one launch (start us, length us, event | category | flops | bytes accessed | tf_op | source)
XLA Modules:
  0.0 58.8 jit_solution(12593888816922745490)
XLA Ops:
  0.6 55.8 %shard_map.67 = (f32[2,4,8,8,128]{4,3,2,1,0:T(8,128)}, f32[3,8,8,1024]{3,2,1,0:T(8,128)}, f32[3,8,8,1024]{3,2,1,0:T(8,128)}) custom-call(s32[8,8,1024]{2,1,0:T(8,128)} %count_in.1, f32[8,8,1024]{2,1,0:T(8,128)} %drag_in.1, f32[3,8,8,1024]{3,2,1,0:T(8,128)} %pvel_in.1, f32[3,8,64,128]{3,2,1,0:T(8,128)} %fluid_in.1), custom_call_target="tpu_custom_call" | custom-call | tf_op jit(solution)/shard_map/pallas_call | solution.py:548
  56.5 2.4 %shard_map.68 = (f32[8,2,4,8,128]{4,3,2,1,0:T(8,128)}, f32[3,8,8,1024]{3,2,1,0:T(8,128)}, f32[3,8,8,1024]{3,2,1,0:T(8,128)}) custom-call(f32[2,4,8,8,128]{4,3,2,1,0:T(8,128)} %get-tuple-element.9.press_in, f32[3,8,8,1024]{3,2,1,0:T(8,128)} %get-tuple-element.10.vel_in, f32[3,8,8,1024]{3,2,1,0:T(8,128)} %get-tuple-element.11.grad_in), custom_call_target="tpu_custom_call" | custom-call | tf_op jit(solution)/shard_map/pallas_call | solution.py:561

commit v8 on v7

--- a/solution.py
+++ b/solution.py
@@ -380,6 +380,50 @@
 
         lax.fori_loop(H + start, H + stop, row, 0, unroll=True)
 
+    def partner(d, back=False):
+        if K & (K - 1) == 0:
+            return chip ^ d
+        return lax.rem(chip + (K - d if back else d), K)
+
+    pieces = ((half - 1, half + 1), (0, half - 1), (half + 1, R))
+    outs, rises = [], []
+
+    def send_piece(i):
+        lo, hi = pieces[i]
+        for d in range(K):
+            for c in range(C):
+                target = partner(d) * C + lax.rem(x + c, C)
+                src = pf.at[H + lo:H + hi, :, pl.ds(pl.multiple_of(target * W, W), W)]
+                dst = rl.at[x, lo:hi]
+                if d == c == 0:
+                    pltpu.make_async_copy(src, dst, out_recv.at[i, x]).start()
+                else:
+                    far = remote(src, dst, out_send.at[i, d * C + c], out_recv.at[i, x], {"gx": target, "gy": k})
+                    outs.append(far)
+                    far.start()
+
+    def rise(i, d):
+        lo, hi = pieces[i]
+        to = partner(d, back=True)
+        for c in range(C):
+            slot = to * C + c
+            remote(
+                pf.at[H + lo:H + hi, :, 0:W], rl.at[slot, lo:hi], out_send.at[i, 0], out_recv.at[i, slot], here
+            ).wait_recv()
+        src, dst = rl.at[pl.ds(to * C, C), lo:hi], press_out.at[:, k, lo:hi]
+        far = remote(src, dst, up_send.at[i, d], up_recv.at[i, k], {"gx": x, "gy": to})
+        near = pltpu.make_async_copy(src, dst, up_recv.at[i, k])
+
+        @pl.when(to != k)
+        def _():
+            far.start()
+
+        @pl.when(to == k)
+        def _():
+            near.start()
+
+        rises.append((to, far))
+
     for j in range(2 - half, H + 1):
         if j == 0:
             arrived(far_counts)
@@ -407,51 +451,20 @@
         if stop > first + 1:
             diagonal(j, first + 1, stop)
 
+    send_piece(0)
     for s in range(ROUNDS[1] - 1, -1, -1):
         arrived(mid_rows(s))
     for l in range(first + 1, last_level + 1):
         rows_of(l, l - last_level, l - H)
 
-    def partner(d, back=False):
-        if K & (K - 1) == 0:
-            return chip ^ d
-        return lax.rem(chip + (K - d if back else d), K)
-
-    outs = []
+    for i in (1, 2):
+        send_piece(i)
+    launch(last_rows())
     for d in range(K):
-        for c in range(C):
-            target = partner(d) * C + lax.rem(x + c, C)
-            src = pf.at[H:H + R, :, pl.ds(pl.multiple_of(target * W, W), W)]
-            if d == c == 0:
-                pltpu.make_async_copy(src, rl.at[x], out_recv.at[x]).start()
-            else:
-                outs.append(remote(src, rl.at[x], out_send.at[d * C + c], out_recv.at[x], {"gx": target, "gy": k}))
-                outs[-1].start()
-
-    launch(last_rows())
-    rises = []
-
-    def rise(d):
-        to = partner(d, back=True)
-        for c in range(C):
-            slot = to * C + c
-            remote(pf.at[H:H + R, :, 0:W], rl.at[slot], out_send.at[0], out_recv.at[slot], here).wait_recv()
-        src = rl.at[pl.ds(to * C, C)]
-        far = remote(src, press_out.at[:, k], up_send.at[d], up_recv.at[k], {"gx": x, "gy": to})
-        near = pltpu.make_async_copy(src, press_out.at[:, k], up_recv.at[k])
-
-        @pl.when(to != k)
-        def _():
-            far.start()
-
-        @pl.when(to == k)
-        def _():
-            near.start()
-
-        rises.append((to, far))
-
+        rise(0, d)
     for d in range(K):
-        rise(d)
+        for i in (1, 2):
+            rise(i, d)
 
     arrived(last_rows())
 
@@ -485,8 +498,11 @@
         def _(far=far):
             far.wait_send()
 
-    for j in range(K):
-        remote(rl.at[0:C], press_out.at[:, j], up_send.at[0], up_recv.at[j], here).wait_recv()
+    for i, (lo, hi) in enumerate(pieces):
+        for j in range(K):
+            remote(
+                rl.at[0:C, lo:hi], press_out.at[:, j, lo:hi], up_send.at[i, 0], up_recv.at[i, j], here
+            ).wait_recv()
     for copy in written:
         copy.wait()
 
@@ -542,7 +558,7 @@
         pltpu.VMEM((G, R, NZ, W), f32),
         dma((4 * NZ,)), dma((2,)), dma((G,)),
         dma((K * C,)), dma((G,)),
-        dma((2, 2)), dma((2, 2)), dma((2, H + 1)), dma((2, H + 1)), dma((2, H)), dma((2, H)), dma((G,)), dma((G,)), dma((K,)), dma((K,)),
+        dma((2, 2)), dma((2, 2)), dma((2, H + 1)), dma((2, H + 1)), dma((2, H)), dma((2, H)), dma((3, G)), dma((3, G)), dma((3, K)), dma((3, K)),
     ]
     anywhere = pl.BlockSpec(memory_space=pl.ANY)
     pressure, velocity, slopes = pl.pallas_call(

time: 59.6 us -> 58.9 us (0.988)
  no operation moved by 1% of the time
where the time goes in v8:
time: 58.9 us; the launch traced here: 58.7 us
  Pallas kernels  58 us (98%)
  between operations  0.64 us (1%)
    pallas_call x1, Pallas kernels, shards(): pl.pallas_call(functools.partial(kernel, K, G, R, NZ, NY, W), out_shape=(...  55.7 us
    pallas_call x1, Pallas kernels, shards(): pl.pallas_call(settle, out_shape=[jax.ShapeDtypeStruct((NZ, C, K, R, W),...  2.35 us

profile of v8, /device:TPU:0, one launch (start us, length us, event | category | flops | bytes accessed | tf_op | source)
XLA Modules:
  0.0 58.7 jit_solution(3592320050888249553)
XLA Ops:
  0.6 55.7 %shard_map.67 = (f32[2,4,8,8,128]{4,3,2,1,0:T(8,128)}, f32[3,8,8,1024]{3,2,1,0:T(8,128)}, f32[3,8,8,1024]{3,2,1,0:T(8,128)}) custom-call(s32[8,8,1024]{2,1,0:T(8,128)} %count_in.1, f32[8,8,1024]{2,1,0:T(8,128)} %drag_in.1, f32[3,8,8,1024]{3,2,1,0:T(8,128)} %pvel_in.1, f32[3,8,64,128]{3,2,1,0:T(8,128)} %fluid_in.1), custom_call_target="tpu_custom_call" | custom-call | tf_op jit(solution)/shard_map/pallas_call | solution.py:564
  56.3 2.4 %shard_map.68 = (f32[8,2,4,8,128]{4,3,2,1,0:T(8,128)}, f32[3,8,8,1024]{3,2,1,0:T(8,128)}, f32[3,8,8,1024]{3,2,1,0:T(8,128)}) custom-call(f32[2,4,8,8,128]{4,3,2,1,0:T(8,128)} %get-tuple-element.9.press_in, f32[3,8,8,1024]{3,2,1,0:T(8,128)} %get-tuple-element.10.vel_in, f32[3,8,8,1024]{3,2,1,0:T(8,128)} %get-tuple-element.11.grad_in), custom_call_target="tpu_custom_call" | custom-call | tf_op jit(solution)/shard_map/pallas_call | solution.py:577

commit v9 on v8

--- a/solution.py
+++ b/solution.py
@@ -371,7 +371,7 @@
             sweep_pair(l, l + (H - j))
             return carry
 
-        lax.fori_loop(start, stop, level, 0)
+        lax.fori_loop(start, stop, level, 0, unroll=True)
 
     def rows_of(l, start, stop):
         def row(lo, carry):
@@ -424,14 +424,15 @@
 
         rises.append((to, far))
 
+    arrived(far_counts)
+    lax.fori_loop(1, H - 1, voids_row, 0)
+    lax.fori_loop(R + H + 1, R + 2 * H - 1, voids_row, 0)
+    wf[1] = 0.5 * (vo[1] + vo[2])
+    lax.fori_loop(2, H, weight_row, 0)
+    lax.fori_loop(R + H, R + 2 * H - 2, weight_row, 0)
+
     for j in range(2 - half, H + 1):
         if j == 0:
-            arrived(far_counts)
-            lax.fori_loop(1, H - 1, voids_row, 0)
-            lax.fori_loop(R + H + 1, R + 2 * H - 1, voids_row, 0)
-            wf[1] = 0.5 * (vo[1] + vo[2])
-            lax.fori_loop(2, H, weight_row, 0)
-            lax.fori_loop(R + H, R + 2 * H - 2, weight_row, 0)
             arrived(flux_rows())
             b[H] = b[H] + fr[0] * rh[H]
             b[H + R - 1] = b[H + R - 1] - fr[1] * rh[H + R - 1]

time: 58.9 us -> 58.8 us (level)
  no operation moved by 1% of the time
where the time goes in v9:
time: 58.8 us; the launch traced here: 58.5 us
  Pallas kernels  57.9 us (98%)
  between operations  0.64 us (1%)
    pallas_call x1, Pallas kernels, shards(): pl.pallas_call(functools.partial(kernel, K, G, R, NZ, NY, W), out_shape=(...  55.5 us
    pallas_call x1, Pallas kernels, shards(): pl.pallas_call(settle, out_shape=[jax.ShapeDtypeStruct((NZ, C, K, R, W),...  2.35 us

profile of v9, /device:TPU:0, one launch (start us, length us, event | category | flops | bytes accessed | tf_op | source)
XLA Modules:
  0.0 58.5 jit_solution(10811262415674275706)
XLA Ops:
  0.6 55.5 %shard_map.67 = (f32[2,4,8,8,128]{4,3,2,1,0:T(8,128)}, f32[3,8,8,1024]{3,2,1,0:T(8,128)}, f32[3,8,8,1024]{3,2,1,0:T(8,128)}) custom-call(s32[8,8,1024]{2,1,0:T(8,128)} %count_in.1, f32[8,8,1024]{2,1,0:T(8,128)} %drag_in.1, f32[3,8,8,1024]{3,2,1,0:T(8,128)} %pvel_in.1, f32[3,8,64,128]{3,2,1,0:T(8,128)} %fluid_in.1), custom_call_target="tpu_custom_call" | custom-call | tf_op jit(solution)/shard_map/pallas_call | solution.py:565
  56.1 2.4 %shard_map.68 = (f32[8,2,4,8,128]{4,3,2,1,0:T(8,128)}, f32[3,8,8,1024]{3,2,1,0:T(8,128)}, f32[3,8,8,1024]{3,2,1,0:T(8,128)}) custom-call(f32[2,4,8,8,128]{4,3,2,1,0:T(8,128)} %get-tuple-element.9.press_in, f32[3,8,8,1024]{3,2,1,0:T(8,128)} %get-tuple-element.10.vel_in, f32[3,8,8,1024]{3,2,1,0:T(8,128)} %get-tuple-element.11.grad_in), custom_call_target="tpu_custom_call" | custom-call | tf_op jit(solution)/shard_map/pallas_call | solution.py:578
